TPU v7x, 128 devices: a whole 4x4x4 slice. The times are simulated.
128 devices in a mesh: group: 16 (over y, z), block: 8 (over x, core).
Axes of the slice: x: 4, y: 4, z: 4, core: 2. Of those that a mesh axis runs over, the one named last changes fastest.
Arguments:
- solution: float32 [16, 64, 5, 16, 256], P('group', 'block'), as said below
- register: float32 [16, 64, 5, 16, 256], P('group', 'block'), may hold values from -1.5 to 1.5
- counts: int32 [8], replicated, may hold values from 1 to 8, 32 in all
Outputs:
- new_solution: float32 [16, 64, 5, 16, 256], P('group', 'block')
- new_register: float32 [16, 64, 5, 16, 256], P('group', 'block')
Inputs may be any that keep to these rules, and one draw needn't show every extreme that they name: `counts`: every index owns at least one block, and some index owns exactly 8 blocks; none owns more. `solution`: each cell in every slot, used or not, holds the conserved variables of a gas state with density between 0.5 and 2 and pressure between 0.5 and 1, with ratio of specific heats 1.4.
All inputs are finite; a program needn't handle non-finite values.
Results may differ from a plain program's by a relative error of at most 0.0003.
Values sent between devices are 32-bit elements; how exact they have to be, the bound alone decides.
A program may use at most 128 MiB of HBM per device.

v0:
```python
import jax
import jax.numpy as jnp
from jax import lax
from jax.sharding import PartitionSpec as P

SECTION = 2


HEAT_RATIO = 1.4
COURANT = 0.5
SERIES_CUT = 0.0001
CENTRAL_WEIGHTS = (0.8, -0.2, 4.0 / 105.0, -1.0 / 280.0)
LOW_STORAGE_A = (
    0.0,
    -567301805773.0 / 1357537059087.0,
    -2404267990393.0 / 2016746695238.0,
    -3550918686646.0 / 2091501179385.0,
    -1275806237668.0 / 842570457699.0,
)
LOW_STORAGE_B = (
    1432997174477.0 / 9575080441755.0,
    5161836677717.0 / 13612068292357.0,
    1720146321549.0 / 2090206949498.0,
    3134564353537.0 / 4481467310338.0,
    2277821191437.0 / 14882151754819.0,
)


def passed_along(value, axis, steps):
    count = lax.axis_size(axis)
    pairs = [(source, (source + steps) % count) for source in range(count)]
    return lax.ppermute(value, axis, pairs)


def primitives(conserved):
    density = conserved[:, 0]
    velocity = conserved[:, 1:4] / density[:, None]
    pressure = (HEAT_RATIO - 1.0) * (
        conserved[:, 4] - 0.5 * jnp.sum(conserved[:, 1:4] * velocity, axis=1)
    )
    return jnp.concatenate(
        [
            density[:, None],
            velocity,
            pressure[:, None],
            jnp.log(density)[:, None],
            jnp.log(pressure)[:, None],
        ],
        axis=1,
    )


def wave_speed(primitive):
    speed_sq = (
        primitive[:, 1] * primitive[:, 1]
        + primitive[:, 2] * primitive[:, 2]
        + primitive[:, 3] * primitive[:, 3]
    )
    return jnp.sqrt(speed_sq) + jnp.sqrt(HEAT_RATIO * primitive[:, 4] / primitive[:, 0])


def squared_ratio_of(first_value, second_value):
    return (first_value * (first_value - 2.0 * second_value) + second_value * second_value) / (
        first_value * (first_value + 2.0 * second_value) + second_value * second_value
    )


def log_mean(first_value, second_value, first_log, second_log):
    ratio_sq = squared_ratio_of(first_value, second_value)
    near_equal = ratio_sq < SERIES_CUT
    series = (first_value + second_value) / (
        2.0 + ratio_sq * (2.0 / 3.0 + ratio_sq * (2.0 / 5.0 + ratio_sq * (2.0 / 7.0)))
    )
    spread = jnp.where(near_equal, 1.0, second_log - first_log)
    return jnp.where(near_equal, series, (second_value - first_value) / spread)


def inverse_log_mean(first_value, second_value, first_log, second_log):
    ratio_sq = squared_ratio_of(first_value, second_value)
    near_equal = ratio_sq < SERIES_CUT
    series = (2.0 + ratio_sq * (2.0 / 3.0 + ratio_sq * (2.0 / 5.0 + ratio_sq * (2.0 / 7.0)))) / (
        first_value + second_value
    )
    spread = jnp.where(near_equal, 1.0, second_value - first_value)
    return jnp.where(near_equal, series, (second_log - first_log) / spread)


def flux_fields(left_side, right_side, direction):
    pressure_left = left_side[:, 4]
    pressure_right = right_side[:, 4]
    density_mean = log_mean(left_side[:, 0], right_side[:, 0], left_side[:, 5], right_side[:, 5])
    inverse_mean = inverse_log_mean(
        left_side[:, 0] * pressure_right,
        right_side[:, 0] * pressure_left,
        left_side[:, 5] + right_side[:, 6],
        right_side[:, 5] + left_side[:, 6],
    )
    averages = [0.5 * (left_side[:, 1 + index] + right_side[:, 1 + index]) for index in range(3)]
    squares = 0.5 * (
        left_side[:, 1] * right_side[:, 1]
        + left_side[:, 2] * right_side[:, 2]
        + left_side[:, 3] * right_side[:, 3]
    )
    pressure_mean = 0.5 * (pressure_left + pressure_right)
    mass_flux = density_mean * averages[direction]
    momenta = []
    for index in range(3):
        if index == direction:
            momenta.append(mass_flux * averages[index] + pressure_mean)
        else:
            momenta.append(mass_flux * averages[index])
    energy_flux = mass_flux * (
        squares + pressure_left * pressure_right * inverse_mean / (HEAT_RATIO - 1.0)
    ) + 0.5 * (
        pressure_left * right_side[:, 1 + direction] + pressure_right * left_side[:, 1 + direction]
    )
    return [mass_flux] + momenta + [energy_flux]


def stepped_fields(primitive, x_lower, x_upper, y_lower, y_upper, z_lower, z_upper, offset):
    edge, lanes = (primitive.shape[2], primitive.shape[3])
    row_ids = lax.broadcasted_iota(jnp.int32, (1, 1, edge, lanes), 2)
    lane_ids = lax.broadcasted_iota(jnp.int32, (1, 1, edge, lanes), 3)
    second_ids = lane_ids // edge
    third_ids = lane_ids % edge
    x_up = jnp.where(
        row_ids < edge - offset,
        jnp.roll(primitive, -offset, axis=2),
        jnp.roll(x_upper, -offset, axis=2),
    )
    x_down = jnp.where(
        row_ids >= offset, jnp.roll(primitive, offset, axis=2), jnp.roll(x_lower, offset, axis=2)
    )
    y_up = jnp.where(
        second_ids < edge - offset,
        jnp.roll(primitive, -offset * edge, axis=3),
        jnp.roll(y_upper, -offset * edge, axis=3),
    )
    y_down = jnp.where(
        second_ids >= offset,
        jnp.roll(primitive, offset * edge, axis=3),
        jnp.roll(y_lower, offset * edge, axis=3),
    )
    z_up = jnp.where(
        third_ids < edge - offset,
        jnp.roll(primitive, -offset, axis=3),
        jnp.roll(z_upper, edge - offset, axis=3),
    )
    z_down = jnp.where(
        third_ids >= offset,
        jnp.roll(primitive, offset, axis=3),
        jnp.roll(z_lower, offset - edge, axis=3),
    )
    return ((x_down, x_up), (y_down, y_up), (z_down, z_up))


def block_tendency(primitive, x_lower, x_upper, y_lower, y_upper, z_lower, z_upper):
    edge, lanes = (primitive.shape[2], primitive.shape[3])
    band = 4 * edge
    x_low_full = jnp.pad(x_lower, ((0, 0), (0, 0), (edge - 4, 0), (0, 0)))
    x_up_full = jnp.pad(x_upper, ((0, 0), (0, 0), (0, edge - 4), (0, 0)))
    y_low_full = jnp.pad(y_lower, ((0, 0), (0, 0), (0, 0), (lanes - band, 0)))
    y_up_full = jnp.pad(y_upper, ((0, 0), (0, 0), (0, 0), (0, lanes - band)))
    summed = [jnp.zeros(primitive[:, 0].shape, jnp.float32) for field in range(5)]
    for offset in range(1, 5):
        factor = 2.0 * CENTRAL_WEIGHTS[offset - 1]
        pairs = stepped_fields(
            primitive, x_low_full, x_up_full, y_low_full, y_up_full, z_lower, z_upper, offset
        )
        for direction in range(3):
            ahead = flux_fields(primitive, pairs[direction][1], direction)
            behind = flux_fields(pairs[direction][0], primitive, direction)
            summed = [summed[field] + factor * (ahead[field] - behind[field]) for field in range(5)]
    return -float(edge) * jnp.stack(summed, axis=1)


def on_device(solution, register, counts):
    blocks = solution[0]
    capacity, edge = (blocks.shape[0], blocks.shape[2])
    lanes = blocks.shape[3]
    band = 4 * edge
    owners = lax.axis_size("block")
    own_index = lax.axis_index("block")
    slot_ids = jnp.arange(capacity, dtype=jnp.int32)
    owned_count = jnp.sum(jnp.where(jnp.arange(owners, dtype=jnp.int32) == own_index, counts, 0))
    occupied = slot_ids < owned_count
    primitive = primitives(blocks)
    local_fastest = jnp.max(jnp.where(occupied[:, None, None], wave_speed(primitive), 0.0))
    fastest = lax.pmax(local_fastest, ("group", "block"))
    time_step = COURANT / (edge * fastest)
    shear_step = lax.axis_size("group") // 4
    x_lower = passed_along(primitive[:, :, edge - 4 :], "group", shear_step)
    x_upper = passed_along(primitive[:, :, :4], "group", -shear_step)
    y_lower = passed_along(primitive[..., lanes - band :], "group", 1)
    y_upper = passed_along(primitive[..., :band], "group", -1)
    last_block = lax.dynamic_index_in_dim(primitive, owned_count - 1, 0, keepdims=False)
    first_block = primitive[0]
    below_run = passed_along(last_block, "block", 1)
    above_run = passed_along(first_block, "block", -1)
    slot_shape = slot_ids[:, None, None, None]
    z_lower = jnp.where(slot_shape == 0, below_run[None], jnp.roll(primitive, 1, axis=0))
    z_upper = jnp.where(
        slot_shape == owned_count - 1, above_run[None], jnp.roll(primitive, -1, axis=0)
    )
    tendency = block_tendency(primitive, x_lower, x_upper, y_lower, y_upper, z_lower, z_upper)
    weight_a = LOW_STORAGE_A[SECTION]
    weight_b = LOW_STORAGE_B[SECTION]
    register_next = weight_a * register[0] + time_step * tendency
    state_next = blocks + weight_b * register_next
    keep = occupied[:, None, None, None]
    new_solution = jnp.where(keep, state_next, 0.0)
    new_register = jnp.where(keep, register_next, 0.0)
    return (new_solution[None], new_register[None])


def solution(mesh):
    in_specs = (P("group", "block", None, None, None), P("group", "block", None, None, None), P())
    out_specs = (P("group", "block", None, None, None), P("group", "block", None, None, None))
    return jax.shard_map(
        on_device, mesh=mesh, in_specs=in_specs, out_specs=out_specs, check_vma=False
    )
```

profile of v0, /device:TPU:1, one launch (start us, length us, event | category | flops | bytes accessed | tf_op | source)
XLA Modules:
  0.0 165.3 jit_solution(3344005982065379293)
XLA Ops:
  5.6 2.6 %collective-permute-start.5 = (f32[7,16,256]{2,1,0:T(8,128)}, f32[7,16,256]{2,1,0:T(8,128)}, u32[]{:S(2)}, u32[]{:S(2)}) collective-permute-start(f32[7,16,256]{2,1,0:T(8,128)} %get-tuple-element.67), channel_id=1, source_target_pairs={{0,1},{1,2},{2,3},{3,4},{4,5},{5,6},{6,7},{7,0},{8,9},{9,10},{10,1... | collective-permute-start | bytes 344072 | tf_op jit(solution)/shard_map/ppermute | solution.py:32
  9.3 1.6 collective-permute-start.3
  11.0 4.6 %collective-permute-start.2 = (f32[8,7,16,64]{3,2,0,1:T(8,128)}, f32[8,7,16,64]{3,2,0,1:T(8,128)S(1)}, u32[]{:S(2)}, u32[]{:S(2)}) collective-permute-start(f32[8,7,16,64]{3,2,0,1:T(8,128)} %get-tuple-element.75), channel_id=1, source_target_pairs={{0,120},{8,0},{16,8},{24,16},{32,24},{40,32},{48,40},{56,48},{64,5... | collective-permute-start | bytes 688136 | tf_op jit(solution)/shard_map/ppermute | solution.py:32
  16.4 1.4 fusion.429
  18.9 1.6 fusion.413
  21.6 1.5 fusion.417
  24.2 1.5 fusion.415
  25.7 1.6 fusion.419
  28.4 1.4 fusion.416
  33.2 1.6 fusion.423
  35.9 1.6 fusion.430
  38.6 1.6 fusion.425
  40.1 1.6 fusion.433
  43.8 1.4 fusion.427
  45.2 1.4 fusion.436
  49.7 65.2 %pmax.7 = f32[]{:T(128)} all-reduce(f32[]{:T(128)} %fusion.408), channel_id=1, replica_groups=mesh['group'=16,'block'=8] {'group','block'}, use_global_device_ids=true, to_apply=%region_3.4 | all-reduce | flops 1 | bytes 8 | tf_op jit(solution)/shard_map/pmax | solution.py:189
  115.6 1.5 collective-permute-start
  142.7 2.0 %maximum_select_fusion.17 = (f32[8,7,16,256]{3,2,0,1:T(8,128)S(1)}, f32[8,7,16,256]{3,2,0,1:T(8,128)S(1)}) fusion(f32[8,7,16,208]{3,2,0,1:T(8,128)S(1)} %copy-done.4, f32[8,7,16,48]{3,2,0,1:T(8,128)S(1)} %copy-done.28, f32[8,7,16,208]{3,2,0,1:T(8,128)S(1)} %pad_slice_fusion.6, f32[8,7,16,48]{3,2,0,1:T(8,128)S(1)} %slice.1583, ...), kind=kLoop, calls=%fused_computation.29 | loop fusion | flops 1146880 | bytes 4825088 | tf_op jit(solution)/shard_map/jit(_where)/select_n | solution.py:139
  144.7 1.8 %maximum_select_fusion.16 = (f32[8,7,16,256]{3,2,0,1:T(8,128)S(1)}, f32[8,7,16,256]{3,2,0,1:T(8,128)S(1)}) fusion(f32[8,7,16,48]{3,2,0,1:T(8,128)S(1)} %copy-done.27, f32[8,7,16,208]{3,2,0,1:T(8,128)S(1)} %copy-done.2, f32[8,7,16,48]{3,2,0,1:T(8,128)S(1)} %bitcast.65, f32[8,7,16,208]{3,2,0,1:T(8,128)S(1)} %pad_slice_fusion.9, ...), kind=kLoop, calls=%fused_computation.28 | loop fusion | flops 1146880 | bytes 4825088 | tf_op jit(solution)/shard_map/jit(_where)/select_n | solution.py:134
  147.2 1.8 %maximum_select_fusion.15 = (f32[8,7,16,256]{3,2,0,1:T(8,128)S(1)}, f32[8,7,16,256]{3,2,0,1:T(8,128)S(1)}) fusion(f32[8,7,13,256]{3,2,0,1:T(8,128)S(1)} %copy-done.12, f32[8,7,3,256]{3,2,0,1:T(4,128)S(1)} %copy-done.42, f32[8,7,13,256]{3,2,0,1:T(8,128)S(1)} %pad_slice_fusion, f32[8,7,3,256]{3,2,0,1:T(4,128)S(1)} %slice.1571, pred[16]{0:T(512)(128)(4,1)S(1)} %copy-done.49, ...), kind=kLoop, calls=%fused_computation.27 | loop fusion | flops 1146880 | bytes 4816928 | tf_op jit(solution)/shard_map/jit(_where)/select_n | solution.py:131
  149.1 1.5 maximum_select_fusion.14
  150.6 3.2 %bitcast_dynamic-update-slice_fusion.3 = (f32[1,8,5,16,256]{4,3,2,1,0:T(8,128)S(1)}, f32[8,1,16,256]{3,2,0,1:T(8,128)S(1)}, f32[8,1,16,256]{3,2,0,1:T(8,128)S(1)...) fusion(f32[8,3,16,256]{3,2,0,1:T(8,128)S(1)} %get-tuple-element, ...), kind=kLoop, calls=%fused_computation.517 | loop fusion | flops 20807680 | bytes 13238272
  156.9 7.0 %bitcast_dynamic-update-slice_fusion.4 = f32[1,8,5,16,256]{4,3,2,1,0:T(8,128)S(1)} fusion(f32[1,8,5,16,256]{4,3,2,1,0:T(8,128)S(1)} %bitcast_dynamic-update-slice_fusion, f32[8,1,16,256]{3,2,0,1:T(8,128)S(1)} %get-tuple-element.25, f32[8,7,16,256]{3,2,0,1:T(8,128)S(1)} %get-tuple-element.120, f32[8,1,16,256]{3,2,0,1:T(8,128)S(1)} %get-tuple-element.26, ...), kind=kLoop, calls=%fused_computation.524 | loop fusion | flops 34897920 | bytes 25952256 | tf_op jit(solution)/shard_map/stack | solution.py:174
  163.9 1.4 broadcast_select_fusion
  (204 shorter events, 49.4 us)
Async XLA Ops:
  5.6 110.0 %collective-permute-start.5 = (f32[7,16,256]{2,1,0:T(8,128)}, f32[7,16,256]{2,1,0:T(8,128)}, u32[]{:S(2)}, u32[]{:S(2)}) collective-permute-start(f32[7,16,256]{2,1,0:T(8,128)} %get-tuple-element.67), channel_id=1, source_target_pairs={{0,1},{1,2},{2,3},{3,4},{4,5},{5,6},{6,7},{7,0},{8,9},{9,10},{10,1... | collective-permute-start | bytes 344072 | tf_op jit(solution)/shard_map/ppermute | solution.py:32
  8.2 111.5 %collective-permute-start.4 = (f32[7,16,256]{2,1,0:T(8,128)}, f32[7,16,256]{2,1,0:T(8,128)}, u32[]{:S(2)}, u32[]{:S(2)}) collective-permute-start(f32[7,16,256]{2,1,0:T(8,128)} %get-tuple-element.65), channel_id=1, source_target_pairs={{0,7},{1,0},{2,1},{3,2},{4,3},{5,4},{6,5},{7,6},{8,15},{9,8},{10,9... | collective-permute-start | bytes 344072 | tf_op jit(solution)/shard_map/ppermute | solution.py:32
  9.3 123.8 %collective-permute-start.3 = (f32[8,7,16,64]{3,2,0,1:T(8,128)}, f32[8,7,16,64]{3,2,0,1:T(8,128)S(1)}, u32[]{:S(2)}, u32[]{:S(2)}) collective-permute-start(f32[8,7,16,64]{3,2,0,1:T(8,128)} %get-tuple-element.76), channel_id=1, source_target_pairs={{0,8},{8,16},{16,24},{24,32},{32,40},{40,48},{48,56},{56,64},{64,7... | collective-permute-start | bytes 688136 | tf_op jit(solution)/shard_map/ppermute | solution.py:32
  11.0 119.7 %collective-permute-start.2 = (f32[8,7,16,64]{3,2,0,1:T(8,128)}, f32[8,7,16,64]{3,2,0,1:T(8,128)S(1)}, u32[]{:S(2)}, u32[]{:S(2)}) collective-permute-start(f32[8,7,16,64]{3,2,0,1:T(8,128)} %get-tuple-element.75), channel_id=1, source_target_pairs={{0,120},{8,0},{16,8},{24,16},{32,24},{40,32},{48,40},{56,48},{64,5... | collective-permute-start | bytes 688136 | tf_op jit(solution)/shard_map/ppermute | solution.py:32
  16.4 122.0 %collective-permute-start.1 = (f32[8,7,4,256]{3,2,0,1:T(4,128)}, f32[8,7,4,256]{3,2,0,1:T(4,128)S(1)}, u32[]{:S(2)}, u32[]{:S(2)}) collective-permute-start(f32[8,7,4,256]{3,2,0,1:T(4,128)} %get-tuple-element.82), channel_id=1, source_target_pairs={{0,32},{8,40},{16,48},{24,56},{32,64},{40,72},{48,80},{56,88},{64,... | collective-permute-start | bytes 688136 | tf_op jit(solution)/shard_map/ppermute | solution.py:32
  48.8 68.3 %copy-start.46 = (f32[1,7,16,256]{3,2,0,1:T(8,128)S(1)}, f32[1,7,16,256]{3,2,0,1:T(8,128)}, u32[]{:S(2)}) copy-start(f32[1,7,16,256]{3,2,0,1:T(8,128)} %get-tuple-element.66) | copy-start | bytes 344068
  115.6 20.6 %collective-permute-start = (f32[8,7,4,256]{3,2,0,1:T(4,128)}, f32[8,7,4,256]{3,2,0,1:T(4,128)S(1)}, u32[]{:S(2)}, u32[]{:S(2)}) collective-permute-start(f32[8,7,4,256]{3,2,0,1:T(4,128)} %get-tuple-element.81), channel_id=1, source_target_pairs={{0,96},{8,104},{16,112},{24,120},{32,0},{40,8},{48,16},{56,24},{64... | collective-permute-start | bytes 688136 | tf_op jit(solution)/shard_map/ppermute | solution.py:32
  119.0 4.0 %copy-start = (f32[8,7,16,256]{3,2,0,1:T(8,128)}, f32[8,7,16,256]{3,2,0,1:T(8,128)S(1)}, u32[]{:S(2)}) copy-start(f32[8,7,16,256]{3,2,0,1:T(8,128)S(1)} %maximum_select_fusion.7) | copy-start | bytes 2752516
  124.3 1.7 %copy-start.32 = (f32[8,7,16,3]{3,2,0,1:T(8,128)S(1)}, f32[8,7,16,3]{3,2,0,1:T(8,128)}, u32[]{:S(2)}) copy-start(f32[8,7,16,3]{3,2,0,1:T(8,128)} %get-tuple-element.43) | copy-start | bytes 32260
  124.3 1.8 %copy-start.33 = (f32[8,7,16,3]{3,2,0,1:T(8,128)S(1)}, f32[8,7,16,3]{3,2,0,1:T(8,128)}, u32[]{:S(2)}) copy-start(f32[8,7,16,3]{3,2,0,1:T(8,128)} %get-tuple-element.44) | copy-start | bytes 32260
  126.1 1.7 %copy-start.39 = (f32[8,7,16,2]{3,2,0,1:T(8,128)S(1)}, f32[8,7,16,2]{3,2,0,1:T(8,128)}, u32[]{:S(2)}) copy-start(f32[8,7,16,2]{3,2,0,1:T(8,128)} %get-tuple-element.55) | copy-start | bytes 21508
  126.1 1.8 %copy-start.40 = (f32[8,7,16,2]{3,2,0,1:T(8,128)S(1)}, f32[8,7,16,2]{3,2,0,1:T(8,128)}, u32[]{:S(2)}) copy-start(f32[8,7,16,2]{3,2,0,1:T(8,128)} %get-tuple-element.56) | copy-start | bytes 21508
  128.0 1.8 %copy-start.38 = (f32[8,7,16,1]{3,2,0,1:T(8,128)S(1)}, f32[8,7,16,1]{3,2,0,1:T(8,128)}, u32[]{:S(2)}) copy-start(f32[8,7,16,1]{3,2,0,1:T(8,128)} %get-tuple-element.74) | copy-start | bytes 10756
  142.7 2.0 %copy-start.1 = (f32[8,7,16,192]{3,2,0,1:T(8,128)S(1)}, f32[8,7,16,192]{3,2,0,1:T(8,128)}, u32[]{:S(2)}) copy-start(f32[8,7,16,192]{3,2,0,1:T(8,128)} %get-tuple-element.37) | copy-start | bytes 2064388
  142.7 2.0 %copy-start.2 = (f32[8,7,16,208]{3,2,0,1:T(8,128)S(1)}, f32[8,7,16,208]{3,2,0,1:T(8,128)}, u32[]{:S(2)}) copy-start(f32[8,7,16,208]{3,2,0,1:T(8,128)} %get-tuple-element.45) | copy-start | bytes 2236420
  142.7 2.0 %copy-start.27 = (f32[8,7,16,48]{3,2,0,1:T(8,128)S(1)}, f32[8,7,16,48]{3,2,0,1:T(8,128)}, u32[]{:S(2)}) copy-start(f32[8,7,16,48]{3,2,0,1:T(8,128)} %get-tuple-element.47) | copy-start | bytes 516100
  144.7 1.9 %copy-start.11 = (f32[8,7,12,256]{3,2,0,1:T(8,128)S(1)}, f32[8,7,12,256]{3,2,0,1:T(8,128)}, u32[]{:S(2)}) copy-start(f32[8,7,12,256]{3,2,0,1:T(8,128)} %get-tuple-element.40) | copy-start | bytes 2064388
  144.7 1.9 %copy-start.12 = (f32[8,7,13,256]{3,2,0,1:T(8,128)S(1)}, f32[8,7,13,256]{3,2,0,1:T(8,128)}, u32[]{:S(2)}) copy-start(f32[8,7,13,256]{3,2,0,1:T(8,128)} %get-tuple-element.50) | copy-start | bytes 2236420
  144.7 1.9 %copy-start.42 = (f32[8,7,3,256]{3,2,0,1:T(4,128)S(1)}, f32[8,7,3,256]{3,2,0,1:T(4,128)}, u32[]{:S(2)}) copy-start(f32[8,7,3,256]{3,2,0,1:T(4,128)} %get-tuple-element.52) | copy-start | bytes 516100
  147.2 1.8 %copy-start.9 = (f32[8,7,12,256]{3,2,0,1:T(8,128)S(1)}, f32[8,7,12,256]{3,2,0,1:T(8,128)}, u32[]{:S(2)}) copy-start(f32[8,7,12,256]{3,2,0,1:T(8,128)} %get-tuple-element.39) | copy-start | bytes 2064388
  147.2 1.8 %copy-start.10 = (f32[8,7,13,256]{3,2,0,1:T(8,128)S(1)}, f32[8,7,13,256]{3,2,0,1:T(8,128)}, u32[]{:S(2)}) copy-start(f32[8,7,13,256]{3,2,0,1:T(8,128)} %get-tuple-element.49) | copy-start | bytes 2236420
  147.2 1.8 %copy-start.41 = (f32[8,7,3,256]{3,2,0,1:T(4,128)S(1)}, f32[8,7,3,256]{3,2,0,1:T(4,128)}, u32[]{:S(2)}) copy-start(f32[8,7,3,256]{3,2,0,1:T(4,128)} %get-tuple-element.51) | copy-start | bytes 516100
  156.8 7.0 %copy-start.26 = (f32[1,8,5,16,256]{4,3,2,1,0:T(8,128)S(1)}, f32[1,8,5,16,256]{4,3,2,1,0:T(8,128)}, u32[]{:S(2)}) copy-start(f32[1,8,5,16,256]{4,3,2,1,0:T(8,128)} %param.3) | copy-start | bytes 1966084
  156.8 7.0 %copy-start.43 = (f32[1,8,5,16,256]{4,3,2,1,0:T(8,128)S(1)}, f32[1,8,5,16,256]{4,3,2,1,0:T(8,128)}, u32[]{:S(2)}) copy-start(f32[1,8,5,16,256]{4,3,2,1,0:T(8,128)} %param.4) | copy-start | bytes 1966084
  (38 other events, 46.2 us)
where the time goes:
time: 166 us; the launch traced here: 165 us
  blocking collectives  65.2 us (39%)
  local copies, waits for them, and re-layouts  51.3 us (31%)
  other arithmetic  34.9 us (21%)
  starting transfers between devices  10.3 us (6%)
  between operations  3.61 us (2%)
    pmax x1, blocking collectives, on_device(): fastest = lax.pmax(local_fastest, ('group', 'block'))  65.2 us
    unnamed x110, local copies, waits for them, and re-layouts  13.8 us
    slice x8, local copies, waits for them, and re-layouts, stepped_fields(): jnp.roll(primitive, -offset, axis=3)  10.7 us
    ppermute x6, starting transfers between devices, passed_along(): return lax.ppermute(value, axis, pairs)  10.3 us
    slice x7, local copies, waits for them, and re-layouts, stepped_fields(): jnp.roll(primitive, -offset * edge, axis=3)  9.44 us
    slice x7, local copies, waits for them, and re-layouts, stepped_fields(): jnp.roll(primitive, -offset, axis=2)  7.91 us
    another operation x1, other arithmetic, block_tendency(): return -float(edge) * jnp.stack(summed, axis=1)  6.98 us
    unnamed x5, other arithmetic  6.27 us
  transfers between devices with their start and end apart: 6, of which 0 were waited for; matrix products, arithmetic and copies ran while one was open for 28% of the time, Pallas kernels for 0%

commit v1 on v0

v1 whole, which is shorter than its diff:
```python
import functools

import jax
import jax.numpy as jnp
from jax import lax
from jax.experimental import pallas as pl
from jax.experimental.pallas import tpu as pltpu
from jax.sharding import PartitionSpec as P

SECTION = 2
HEAT_RATIO = 1.4
COURANT = 0.5
SERIES_CUT = 0.0001
CENTRAL_WEIGHTS = (0.8, -0.2, 4.0 / 105.0, -1.0 / 280.0)
LOW_STORAGE_A = (
    0.0,
    -567301805773.0 / 1357537059087.0,
    -2404267990393.0 / 2016746695238.0,
    -3550918686646.0 / 2091501179385.0,
    -1275806237668.0 / 842570457699.0,
)
LOW_STORAGE_B = (
    1432997174477.0 / 9575080441755.0,
    5161836677717.0 / 13612068292357.0,
    1720146321549.0 / 2090206949498.0,
    3134564353537.0 / 4481467310338.0,
    2277821191437.0 / 14882151754819.0,
)
MESH = pl.DeviceIdType.MESH
EDGE = 16
CAP = 8
LANES = 128
FIELDS = 8


def cell_fields(state):
    density, first, second, third, energy = state
    inverse = 1.0 / density
    v1, v2, v3 = first * inverse, second * inverse, third * inverse
    pressure = (HEAT_RATIO - 1.0) * (energy - 0.5 * (first * v1 + second * v2 + third * v3))
    half_log = 0.5 * jnp.log(density)
    half_log_p = 0.5 * jnp.log(pressure)
    fields = [
        0.5 * density,
        0.5 * v1,
        0.5 * v2,
        0.5 * v3,
        0.5 * pressure,
        half_log,
        (HEAT_RATIO - 1.0) * (density / pressure),
        half_log - half_log_p,
    ]
    return fields, (v1, v2, v3, pressure, inverse)


def mean_parts(left, right, left_log, right_log):
    total = left + right
    step = right - left
    ratio = step / total
    ratio_sq = ratio * ratio
    near = ratio_sq < SERIES_CUT
    series = 1.0 + ratio_sq * (1.0 / 3.0 + ratio_sq * (1.0 / 5.0 + ratio_sq * (1.0 / 7.0)))
    return jnp.where(near, total, step), jnp.where(near, series, right_log - left_log)


def pair_flux(left, right, direction, factor):
    means = [left[1 + m] + right[1 + m] for m in range(3)]
    products = left[1] * right[1] + left[2] * right[2] + left[3] * right[3]
    top, bottom = mean_parts(left[0], right[0], left[5], right[5])
    top_t, bottom_t = mean_parts(left[6], right[6], left[7], right[7])
    mass = (top / bottom) * (factor * means[direction])
    inverse_mean = bottom_t / top_t
    momenta = [mass * means[m] for m in range(3)]
    momenta[direction] = momenta[direction] + factor * (left[4] + right[4])
    cross = left[4] * right[1 + direction] + right[4] * left[1 + direction]
    energy = mass * (products + inverse_mean) + factor * cross
    return [mass] + momenta + [energy]


FACTORS = tuple(-float(EDGE) * 2.0 * weight for weight in CENTRAL_WEIGHTS)


def tendency_kernel(
    counts_ref,
    sol_hbm,
    out_ref,
    sol,
    cons,
    pack_x,
    pack_z,
    halo_x,
    halo_y,
    halo_z,
    nat,
    tra,
    line_flux,
    plane_flux,
    tend_x,
    tend_t,
    peak,
    peak_in,
    load_sem,
    send_sem,
    recv_sem,
    peak_send,
    peak_recv,
):
    g = lax.axis_index("group")
    b = lax.axis_index("block")
    groups = lax.axis_size("group")
    owners = lax.axis_size("block")
    shear = groups // 4
    zdim = groups // shear
    base = (g // zdim) * zdim
    block_peers = [(g, lax.rem(b + j, owners)) for j in range(1, owners)]
    y_peers = [(lax.rem(g + shear * j, groups), b) for j in range(1, 4)]
    z_peers = [(base + lax.rem(g - base + j, zdim), b) for j in range(1, zdim)]
    up_y, down_y = (lax.rem(g + 1, groups), b), (lax.rem(g + groups - 1, groups), b)
    up_x, down_x = y_peers[0], y_peers[2]
    up_z, down_z = block_peers[0], block_peers[-1]

    load = pltpu.make_async_copy(sol_hbm, sol, load_sem)
    load.start()
    barrier = pltpu.get_barrier_semaphore()
    everyone = block_peers + y_peers + z_peers + [up_y, down_y]
    for peer in everyone:
        pl.semaphore_signal(barrier, inc=1, device_id=peer, device_id_type=MESH)
    load.wait()

    for f in range(5):
        for s in range(CAP):
            pack_x[0, f, 4 * s : 4 * s + 4, :] = sol[s, f, 0:4, :]
            pack_x[1, f, 4 * s : 4 * s + 4, :] = sol[s, f, EDGE - 4 : EDGE, :]
    for f in range(5):
        for half in range(2):
            part = sol[:, f, :, half * LANES : (half + 1) * LANES].reshape(LANES, LANES)
            cons[f, half * 8 : (half + 1) * 8, :, :] = part.T.reshape(8, EDGE, LANES)
    for f in range(5):
        for y in range(EDGE):
            pack_z[0, f, 4 * y : 4 * y + 4, :] = cons[f, y, 0:4, :]
            pack_z[1, f, 4 * y : 4 * y + 4, :] = cons[f, y, EDGE - 4 : EDGE, :]

    pl.semaphore_wait(barrier, len(everyone))

    def send(index, source, target, peer):
        copy = pltpu.make_async_remote_copy(
            src_ref=source,
            dst_ref=target,
            send_sem=send_sem.at[index],
            recv_sem=recv_sem.at[index],
            device_id=peer,
            device_id_type=MESH,
        )
        copy.start()
        return copy

    copies = [
        send(0, pack_z.at[1], halo_z.at[0], up_z),
        send(1, pack_z.at[0], halo_z.at[1], down_z),
        send(2, pack_x.at[1], halo_x.at[0], up_x),
        send(3, pack_x.at[0], halo_x.at[1], down_x),
        send(4, cons.at[:, EDGE - 4 : EDGE], halo_y.at[0], up_y),
        send(5, cons.at[:, 0:4], halo_y.at[1], down_y),
    ]

    owned = counts_ref[b]
    owned_below = counts_ref[lax.rem(b + owners - 1, owners)]
    lane_slot = lax.broadcasted_iota(jnp.int32, (8, LANES), 1) // EDGE

    def transposed_fields(y, fastest):
        for zt in range(2):
            rows = slice(8 * zt, 8 * zt + 8)
            fields, (v1, v2, v3, pressure, inverse) = cell_fields(
                [cons[f, y, rows, :] for f in range(5)]
            )
            for f in range(FIELDS):
                tra[f, y + 4, 8 + 8 * zt : 16 + 8 * zt, :] = fields[f]
            speed = jnp.sqrt(v1 * v1 + v2 * v2 + v3 * v3) + jnp.sqrt(
                HEAT_RATIO * pressure * inverse
            )
            fastest = jnp.maximum(fastest, speed)
        return fastest

    fastest = lax.fori_loop(0, EDGE, transposed_fields, jnp.zeros((8, LANES), jnp.float32))
    peak[0] = jnp.where(lane_slot < owned, fastest, 0.0)

    def natural_fields(s, carry):
        for half in range(2):
            for rt in range(2):
                fields, _ = cell_fields(
                    [
                        sol[s, f, 8 * rt : 8 * rt + 8, half * LANES : (half + 1) * LANES]
                        for f in range(5)
                    ]
                )
                for f in range(FIELDS):
                    nat[f, 2 * s + half, 8 + 8 * rt : 16 + 8 * rt, :] = fields[f]
        return carry

    lax.fori_loop(0, CAP, natural_fields, 0)

    def exchange_peaks(stage, first, peers):
        started = []
        for j, peer in enumerate(peers):
            copy = pltpu.make_async_remote_copy(
                src_ref=peak.at[stage],
                dst_ref=peak_in.at[first + j],
                send_sem=peak_send.at[first + j],
                recv_sem=peak_recv.at[first + j],
                device_id=peer,
                device_id_type=MESH,
            )
            copy.start()
            started.append(copy)
        return started

    def gather_peaks(stage, first, started):
        value = peak[stage]
        for j, copy in enumerate(started):
            copy.wait()
            value = jnp.maximum(value, peak_in[first + j])
        return value

    block_copies = exchange_peaks(0, 0, block_peers)

    def line_tendency(ref, line, direction, store):
        left = [
            [ref[f, line, 8 + 8 * c : 16 + 8 * c, :] for f in range(FIELDS)] for c in range(2)
        ]
        low = [ref[f, line, 4:8, :] for f in range(FIELDS)]
        total = [[None] * 5 for c in range(2)]
        for k in range(1, 5):
            below = pair_flux(
                low, [ref[f, line, 4 + k : 8 + k, :] for f in range(FIELDS)], direction, FACTORS[k - 1]
            )
            for f in range(5):
                line_flux[k - 1, f, 4:8, :] = below[f]
            for c in range(2):
                at = 8 + 8 * c
                flux = pair_flux(
                    left[c],
                    [ref[f, line, at + k : at + 8 + k, :] for f in range(FIELDS)],
                    direction,
                    FACTORS[k - 1],
                )
                for f in range(5):
                    line_flux[k - 1, f, at : at + 8, :] = flux[f]
                    total[c][f] = flux[f] if k == 1 else total[c][f] + flux[f]
            for c in range(2):
                at = 8 + 8 * c
                for f in range(5):
                    total[c][f] = total[c][f] - line_flux[k - 1, f, at - k : at + 8 - k, :]
        for c in range(2):
            for f in range(5):
                store(f, c, total[c][f])

    copies[0].wait_recv()
    copies[1].wait_recv()

    def third_halo(i, carry):
        rows = pl.ds(pl.multiple_of(8 * i, 8), 8)
        lower, upper = [], []
        for f in range(5):
            below = jnp.where(lane_slot == owned_below - 1, halo_z[0, f, rows, :], 0.0)
            above = jnp.where(lane_slot == 0, halo_z[1, f, rows, :], 0.0)
            for shift in (16, 32, 64):
                below = below + pltpu.roll(below, shift, 1)
                above = above + pltpu.roll(above, shift, 1)
            lower.append(
                jnp.where(lane_slot == 0, below, pltpu.roll(pack_z[1, f, rows, :], EDGE, 1))
            )
            upper.append(
                jnp.where(
                    lane_slot == owned - 1, above, pltpu.roll(pack_z[0, f, rows, :], LANES - EDGE, 1)
                )
            )
        lower, _ = cell_fields(lower)
        upper, _ = cell_fields(upper)
        for f in range(FIELDS):
            for j in range(2):
                tra[f, 2 * i + j + 4, 4:8, :] = lower[f][4 * j : 4 * j + 4]
                tra[f, 2 * i + j + 4, 24:28, :] = upper[f][4 * j : 4 * j + 4]
        return carry

    lax.fori_loop(0, EDGE // 2, third_halo, 0)

    def third_line(y, carry):
        def store(f, c, value):
            tend_t[f, y, 8 * c : 8 * c + 8, :] = value

        line_tendency(tra, y + 4, 2, store)
        return carry

    lax.fori_loop(0, EDGE, third_line, 0)

    peak[1] = gather_peaks(0, 0, block_copies)
    y_copies = exchange_peaks(1, owners - 1, y_peers)

    def plane_pair(y, k, zt):
        rows = slice(8 + 8 * zt, 16 + 8 * zt)
        return pair_flux(
            [tra[f, y + 4, rows, :] for f in range(FIELDS)],
            [tra[f, y + 4 + k, rows, :] for f in range(FIELDS)],
            1,
            FACTORS[k - 1],
        )

    def ahead(y, offsets):
        for zt in range(2):
            rows = slice(8 * zt, 8 * zt + 8)
            total = [tend_t[f, y, rows, :] for f in range(5)]
            for k in offsets:
                flux = plane_pair(y, k, zt)
                for f in range(5):
                    plane_flux[k - 1, f, y + 4, rows, :] = flux[f]
                    total[f] = total[f] + flux[f]
            for f in range(5):
                tend_t[f, y, rows, :] = total[f]

    def second_interior(y, carry):
        ahead(y, range(1, 5))
        return carry

    lax.fori_loop(0, EDGE - 4, second_interior, 0)
    for y in range(EDGE - 4, EDGE - 1):
        ahead(y, range(1, EDGE - y))

    copies[2].wait_recv()
    copies[3].wait_recv()

    def first_halo(i, carry):
        rows = pl.ds(pl.multiple_of(8 * i, 8), 8)
        for side in range(2):
            at = 4 if side == 0 else 24
            for half in range(2):
                lanes = slice(half * LANES, (half + 1) * LANES)
                fields, _ = cell_fields([halo_x[side, f, rows, lanes] for f in range(5)])
                for f in range(FIELDS):
                    for j in range(2):
                        nat[f, 2 * (2 * i + j) + half, at : at + 4, :] = fields[f][4 * j : 4 * j + 4]
        return carry

    lax.fori_loop(0, CAP // 2, first_halo, 0)

    def first_line(line, carry):
        def store(f, c, value):
            tend_x[f, line, 8 * c : 8 * c + 8, :] = value

        line_tendency(nat, line, 0, store)
        return carry

    lax.fori_loop(0, 2 * CAP, first_line, 0)

    peak[2] = gather_peaks(1, owners - 1, y_copies)
    z_copies = exchange_peaks(2, owners + 2, z_peers)

    copies[4].wait_recv()
    copies[5].wait_recv()

    def second_halo(y, carry):
        for side in range(2):
            for zt in range(2):
                rows = slice(8 * zt, 8 * zt + 8)
                fields, _ = cell_fields([halo_y[side, f, y, rows, :] for f in range(5)])
                for f in range(FIELDS):
                    tra[f, y + 20 * side, 8 + 8 * zt : 16 + 8 * zt, :] = fields[f]
        return carry

    lax.fori_loop(0, 4, second_halo, 0)
    for y in range(-4, 0):
        for k in range(-y, 5):
            for zt in range(2):
                flux = plane_pair(y, k, zt)
                for f in range(5):
                    plane_flux[k - 1, f, y + 4, 8 * zt : 8 * zt + 8, :] = flux[f]
    for y in range(EDGE - 4, EDGE):
        ahead(y, range(EDGE - y, 5))

    def behind(y, carry):
        for zt in range(2):
            rows = slice(8 * zt, 8 * zt + 8)
            for f in range(5):
                total = tend_t[f, y, rows, :]
                for k in range(1, 5):
                    total = total - plane_flux[k - 1, f, y + 4 - k, rows, :]
                tend_t[f, y, rows, :] = total
        return carry

    lax.fori_loop(0, EDGE, behind, 0)

    top = jnp.max(gather_peaks(2, owners + 2, z_copies), keepdims=True)
    time_step = COURANT / (EDGE * top)
    for f in range(5):
        scale = 2.0 * time_step if f == 4 else time_step
        for half in range(2):
            part = tend_t[f, half * 8 : (half + 1) * 8, :, :].reshape(LANES, LANES).T
            for s in range(CAP):
                out_ref[s, f, :, half * LANES : (half + 1) * LANES] = scale * (
                    part[s * EDGE : (s + 1) * EDGE] + tend_x[f, 2 * s + half, :, :]
                )
    for copy in copies:
        copy.wait_send()


def update_kernel(counts_ref, step_ref, sol_ref, reg_ref, new_sol_ref, new_reg_ref):
    owned = counts_ref[lax.axis_index("block")]
    size = step_ref.shape[0]
    first = pl.program_id(0) * size
    for s in range(size):
        keep = first + s < owned
        register = LOW_STORAGE_A[SECTION] * reg_ref[s] + step_ref[s]
        state = sol_ref[s] + LOW_STORAGE_B[SECTION] * register
        new_reg_ref[s] = jnp.where(keep, register, 0.0)
        new_sol_ref[s] = jnp.where(keep, state, 0.0)


def on_device(solution, register, counts):
    blocks, old_register = solution[0], register[0]
    shape = blocks.shape
    f32 = jnp.float32
    scratch = [
        pltpu.VMEM(shape, f32),
        pltpu.VMEM((5, EDGE, EDGE, LANES), f32),
        pltpu.VMEM((2, 5, 4 * CAP, 2 * LANES), f32),
        pltpu.VMEM((2, 5, 4 * EDGE, LANES), f32),
        pltpu.VMEM((2, 5, 4 * CAP, 2 * LANES), f32),
        pltpu.VMEM((2, 5, 4, EDGE, LANES), f32),
        pltpu.VMEM((2, 5, 4 * EDGE, LANES), f32),
        pltpu.VMEM((FIELDS, 2 * CAP, 32, LANES), f32),
        pltpu.VMEM((FIELDS, EDGE + 8, 32, LANES), f32),
        pltpu.VMEM((4, 5, 24, LANES), f32),
        pltpu.VMEM((4, 5, EDGE + 4, EDGE, LANES), f32),
        pltpu.VMEM((5, 2 * CAP, EDGE, LANES), f32),
        pltpu.VMEM((5, EDGE, EDGE, LANES), f32),
        pltpu.VMEM((3, 8, LANES), f32),
        pltpu.VMEM((13, 8, LANES), f32),
        pltpu.SemaphoreType.DMA,
        pltpu.SemaphoreType.DMA((6,)),
        pltpu.SemaphoreType.DMA((6,)),
        pltpu.SemaphoreType.DMA((13,)),
        pltpu.SemaphoreType.DMA((13,)),
    ]
    step = pl.pallas_call(
        tendency_kernel,
        out_shape=jax.ShapeDtypeStruct(shape, f32),
        in_specs=[
            pl.BlockSpec(memory_space=pltpu.SMEM),
            pl.BlockSpec(memory_space=pl.ANY),
        ],
        out_specs=pl.BlockSpec(memory_space=pltpu.VMEM),
        scratch_shapes=scratch,
        compiler_params=pltpu.CompilerParams(
            collective_id=0, has_side_effects=True, vmem_limit_bytes=40 * 2**20
        ),
        name="tendency",
    )(counts, blocks)
    size = 2
    spec = pl.BlockSpec((size,) + shape[1:], lambda i: (i, 0, 0, 0))
    new_solution, new_register = pl.pallas_call(
        update_kernel,
        grid=(CAP // size,),
        out_shape=[jax.ShapeDtypeStruct(shape, f32)] * 2,
        in_specs=[pl.BlockSpec(memory_space=pltpu.SMEM), spec, spec, spec],
        out_specs=[spec, spec],
        name="update",
    )(counts, step, blocks, old_register)
    return (new_solution[None], new_register[None])


def solution(mesh):
    in_specs = (P("group", "block", None, None, None), P("group", "block", None, None, None), P())
    out_specs = (P("group", "block", None, None, None), P("group", "block", None, None, None))
    return jax.shard_map(
        on_device, mesh=mesh, in_specs=in_specs, out_specs=out_specs, check_vma=False
    )
```

time: 166 us -> 30 us (0.18)
  the two profiles are of different devices: /device:TPU:1 before, /device:TPU:0 now
where the time goes in v1:
time: 30 us; the launch traced here: 29.7 us
  Pallas kernels  26.5 us (88%)
  local copies, waits for them, and re-layouts  2.57 us (9%)
  between operations  0.65 us (2%)
    pallas_call x1, Pallas kernels, on_device(): pl.pallas_call(tendency_kernel, out_shape=jax.ShapeDtypeStruct(shape, f32...  22.8 us
    pallas_call x1, Pallas kernels, on_device(): pl.pallas_call(update_kernel, grid=(CAP // size,), out_shape=[jax.ShapeDt...  3.69 us
    unnamed x6, local copies, waits for them, and re-layouts  2.57 us

profile of v1, /device:TPU:0, one launch (start us, length us, event | category | flops | bytes accessed | tf_op | source)
XLA Modules:
  0.0 29.7 jit_solution(9895849364573622737)
XLA Ops:
  0.6 0.0 copy-start.2
  0.6 0.6 %copy-done.2 = s32[8]{0:T(128)S(1)} copy-done((s32[8]{0:T(128)S(1)}, s32[8]{0:T(128)}, u32[]{:S(2)}) %copy-start.2) | copy-done | bytes 56
  1.3 0.0 copy-start
  1.3 1.1 %copy-done = f32[1,8,5,16,256]{4,3,2,1,0:T(8,128)S(1)} copy-done((f32[1,8,5,16,256]{4,3,2,1,0:T(8,128)S(1)}, f32[1,8,5,16,256]{4,3,2,1,0:T(8,128)}, u32[]{:S(2)}) %copy-start) | copy-done | bytes 655384
  2.4 22.8 %tendency.1.step_ref = f32[8,5,16,256]{3,2,1,0:T(8,128)S(1)} custom-call(s32[8]{0:T(128)S(1)} %copy-done.2, f32[8,5,16,256]{3,2,1,0:T(8,128)S(1)} %bitcast.5), custom_call_target="tpu_custom_call" | custom-call | tf_op jit(solution)/shard_map/tendency/pallas_call | solution.py:443
  25.2 0.0 copy-start.1
  25.2 0.8 %copy-done.1 = f32[8,5,16,256]{3,2,1,0:T(8,128)} copy-done((f32[8,5,16,256]{3,2,1,0:T(8,128)}, f32[8,5,16,256]{3,2,1,0:T(8,128)S(1)}, u32[]{:S(2)}) %copy-start.1) | copy-done | bytes 655384
  26.0 3.7 %update.1 = (f32[8,5,16,256]{3,2,1,0:T(8,128)}, f32[8,5,16,256]{3,2,1,0:T(8,128)}) custom-call(s32[8]{0:T(128)} %counts_ref.3, f32[8,5,16,256]{3,2,1,0:T(8,128)} %copy-done.1, f32[8,5,16,256]{3,2,1,0:T(8,128)} %bitcast.4, f32[8,5,16,256]{3,2,1,0:T(8,128)} %bitcast.6), custom_call_target="tpu_custom_call" | custom-call | tf_op jit(solution)/shard_map/update/pallas_call | solution.py:459
Async XLA Ops:
  0.6 0.7 %copy-start.2 = (s32[8]{0:T(128)S(1)}, s32[8]{0:T(128)}, u32[]{:S(2)}) copy-start(s32[8]{0:T(128)} %counts_ref.3) | copy-start | bytes 100
  1.3 1.1 %copy-start = (f32[1,8,5,16,256]{4,3,2,1,0:T(8,128)S(1)}, f32[1,8,5,16,256]{4,3,2,1,0:T(8,128)}, u32[]{:S(2)}) copy-start(f32[1,8,5,16,256]{4,3,2,1,0:T(8,128)} %param.3) | copy-start | bytes 1966084
  25.2 0.8 %copy-start.1 = (f32[8,5,16,256]{3,2,1,0:T(8,128)}, f32[8,5,16,256]{3,2,1,0:T(8,128)S(1)}, u32[]{:S(2)}) copy-start(f32[8,5,16,256]{3,2,1,0:T(8,128)S(1)} %tendency.1.step_ref) | copy-start | bytes 1966084

commit v2 on v1

--- a/solution.py
+++ b/solution.py
@@ -29,6 +29,7 @@
 MESH = pl.DeviceIdType.MESH
 EDGE = 16
 CAP = 8
+OWNERS = 8
 LANES = 128
 FIELDS = 8
 
@@ -81,10 +82,14 @@
 
 
 def tendency_kernel(
+    counts_hbm,
+    sol_hbm,
+    reg_hbm,
+    out_ref,
+    info_ref,
+    sol,
+    reg,
     counts_ref,
-    sol_hbm,
-    out_ref,
-    sol,
     cons,
     pack_x,
     pack_z,
@@ -100,6 +105,8 @@
     peak,
     peak_in,
     load_sem,
+    counts_sem,
+    reg_sem,
     send_sem,
     recv_sem,
     peak_send,
@@ -119,13 +126,41 @@
     up_x, down_x = y_peers[0], y_peers[2]
     up_z, down_z = block_peers[0], block_peers[-1]
 
+    counts_load = pltpu.make_async_copy(counts_hbm, counts_ref, counts_sem)
+    counts_load.start()
     load = pltpu.make_async_copy(sol_hbm, sol, load_sem)
     load.start()
     barrier = pltpu.get_barrier_semaphore()
-    everyone = block_peers + y_peers + z_peers + [up_y, down_y]
+    everyone = [up_y, down_y] + y_peers + z_peers + block_peers
     for peer in everyone:
         pl.semaphore_signal(barrier, inc=1, device_id=peer, device_id_type=MESH)
+    reg_load = pltpu.make_async_copy(reg_hbm, reg, reg_sem)
+    reg_load.start()
+    counts_load.wait()
+    owned = counts_ref[b]
+    owned_below = counts_ref[lax.rem(b + owners - 1, owners)]
+    lane_slot = lax.broadcasted_iota(jnp.int32, (8, LANES), 1) // EDGE
     load.wait()
+
+    def natural_fields(s, fastest):
+        used = jnp.full((8, LANES), s, jnp.int32) < owned
+        for half in range(2):
+            for rt in range(2):
+                fields, (v1, v2, v3, pressure, inverse) = cell_fields(
+                    [
+                        sol[s, f, 8 * rt : 8 * rt + 8, half * LANES : (half + 1) * LANES]
+                        for f in range(5)
+                    ]
+                )
+                for f in range(FIELDS):
+                    nat[f, 2 * s + half, 8 + 8 * rt : 16 + 8 * rt, :] = fields[f]
+                speed = jnp.sqrt(v1 * v1 + v2 * v2 + v3 * v3) + jnp.sqrt(
+                    HEAT_RATIO * pressure * inverse
+                )
+                fastest = jnp.maximum(fastest, jnp.where(used, speed, 0.0))
+        return fastest
+
+    peak[0] = lax.fori_loop(0, CAP, natural_fields, jnp.zeros((8, LANES), jnp.float32))
 
     for f in range(5):
         for s in range(CAP):
@@ -139,65 +174,6 @@
         for y in range(EDGE):
             pack_z[0, f, 4 * y : 4 * y + 4, :] = cons[f, y, 0:4, :]
             pack_z[1, f, 4 * y : 4 * y + 4, :] = cons[f, y, EDGE - 4 : EDGE, :]
-
-    pl.semaphore_wait(barrier, len(everyone))
-
-    def send(index, source, target, peer):
-        copy = pltpu.make_async_remote_copy(
-            src_ref=source,
-            dst_ref=target,
-            send_sem=send_sem.at[index],
-            recv_sem=recv_sem.at[index],
-            device_id=peer,
-            device_id_type=MESH,
-        )
-        copy.start()
-        return copy
-
-    copies = [
-        send(0, pack_z.at[1], halo_z.at[0], up_z),
-        send(1, pack_z.at[0], halo_z.at[1], down_z),
-        send(2, pack_x.at[1], halo_x.at[0], up_x),
-        send(3, pack_x.at[0], halo_x.at[1], down_x),
-        send(4, cons.at[:, EDGE - 4 : EDGE], halo_y.at[0], up_y),
-        send(5, cons.at[:, 0:4], halo_y.at[1], down_y),
-    ]
-
-    owned = counts_ref[b]
-    owned_below = counts_ref[lax.rem(b + owners - 1, owners)]
-    lane_slot = lax.broadcasted_iota(jnp.int32, (8, LANES), 1) // EDGE
-
-    def transposed_fields(y, fastest):
-        for zt in range(2):
-            rows = slice(8 * zt, 8 * zt + 8)
-            fields, (v1, v2, v3, pressure, inverse) = cell_fields(
-                [cons[f, y, rows, :] for f in range(5)]
-            )
-            for f in range(FIELDS):
-                tra[f, y + 4, 8 + 8 * zt : 16 + 8 * zt, :] = fields[f]
-            speed = jnp.sqrt(v1 * v1 + v2 * v2 + v3 * v3) + jnp.sqrt(
-                HEAT_RATIO * pressure * inverse
-            )
-            fastest = jnp.maximum(fastest, speed)
-        return fastest
-
-    fastest = lax.fori_loop(0, EDGE, transposed_fields, jnp.zeros((8, LANES), jnp.float32))
-    peak[0] = jnp.where(lane_slot < owned, fastest, 0.0)
-
-    def natural_fields(s, carry):
-        for half in range(2):
-            for rt in range(2):
-                fields, _ = cell_fields(
-                    [
-                        sol[s, f, 8 * rt : 8 * rt + 8, half * LANES : (half + 1) * LANES]
-                        for f in range(5)
-                    ]
-                )
-                for f in range(FIELDS):
-                    nat[f, 2 * s + half, 8 + 8 * rt : 16 + 8 * rt, :] = fields[f]
-        return carry
-
-    lax.fori_loop(0, CAP, natural_fields, 0)
 
     def exchange_peaks(stage, first, peers):
         started = []
@@ -221,7 +197,40 @@
             value = jnp.maximum(value, peak_in[first + j])
         return value
 
+    pl.semaphore_wait(barrier, len(everyone))
     block_copies = exchange_peaks(0, 0, block_peers)
+
+    def send(index, source, target, peer):
+        copy = pltpu.make_async_remote_copy(
+            src_ref=source,
+            dst_ref=target,
+            send_sem=send_sem.at[index],
+            recv_sem=recv_sem.at[index],
+            device_id=peer,
+            device_id_type=MESH,
+        )
+        copy.start()
+        return copy
+
+    copies = [
+        send(0, pack_z.at[1], halo_z.at[0], up_z),
+        send(1, pack_z.at[0], halo_z.at[1], down_z),
+        send(2, pack_x.at[1], halo_x.at[0], up_x),
+        send(3, pack_x.at[0], halo_x.at[1], down_x),
+        send(4, cons.at[:, EDGE - 4 : EDGE], halo_y.at[0], up_y),
+        send(5, cons.at[:, 0:4], halo_y.at[1], down_y),
+    ]
+
+    def transposed_fields(y, carry):
+        for zt in range(2):
+            rows = slice(8 * zt, 8 * zt + 8)
+            fields = cell_fields([cons[f, y, rows, :] for f in range(5)])[0]
+            for f in range(FIELDS):
+                tra[f, y + 4, 8 + 8 * zt : 16 + 8 * zt, :] = fields[f]
+        return carry
+
+    lax.fori_loop(0, EDGE, transposed_fields, 0)
+
 
     def line_tendency(ref, line, direction, store):
         left = [
@@ -254,6 +263,37 @@
             for f in range(5):
                 store(f, c, total[c][f])
 
+    def plane_pair(y, k, zt):
+        rows = slice(8 + 8 * zt, 16 + 8 * zt)
+        return pair_flux(
+            [tra[f, y + 4, rows, :] for f in range(FIELDS)],
+            [tra[f, y + 4 + k, rows, :] for f in range(FIELDS)],
+            1,
+            FACTORS[k - 1],
+        )
+
+    def ahead(y, offsets, fresh):
+        for zt in range(2):
+            rows = slice(8 * zt, 8 * zt + 8)
+            total = [None if fresh else tend_t[f, y, rows, :] for f in range(5)]
+            for k in offsets:
+                flux = plane_pair(y, k, zt)
+                for f in range(5):
+                    plane_flux[k - 1, f, y + 4, rows, :] = flux[f]
+                    total[f] = flux[f] if total[f] is None else total[f] + flux[f]
+            for f in range(5):
+                tend_t[f, y, rows, :] = total[f]
+
+    def second_interior(y, carry):
+        ahead(y, range(1, 5), True)
+        return carry
+
+    lax.fori_loop(0, EDGE - 4, second_interior, 0)
+    for y in range(EDGE - 4, EDGE - 1):
+        ahead(y, range(1, EDGE - y), True)
+    for f in range(5):
+        tend_t[f, EDGE - 1, :, :] = jnp.zeros((EDGE, LANES), jnp.float32)
+
     copies[0].wait_recv()
     copies[1].wait_recv()
 
@@ -286,44 +326,16 @@
 
     def third_line(y, carry):
         def store(f, c, value):
-            tend_t[f, y, 8 * c : 8 * c + 8, :] = value
+            rows = slice(8 * c, 8 * c + 8)
+            tend_t[f, y, rows, :] = tend_t[f, y, rows, :] + value
 
         line_tendency(tra, y + 4, 2, store)
         return carry
 
-    lax.fori_loop(0, EDGE, third_line, 0)
-
+    lax.fori_loop(0, EDGE // 2, third_line, 0)
     peak[1] = gather_peaks(0, 0, block_copies)
-    y_copies = exchange_peaks(1, owners - 1, y_peers)
-
-    def plane_pair(y, k, zt):
-        rows = slice(8 + 8 * zt, 16 + 8 * zt)
-        return pair_flux(
-            [tra[f, y + 4, rows, :] for f in range(FIELDS)],
-            [tra[f, y + 4 + k, rows, :] for f in range(FIELDS)],
-            1,
-            FACTORS[k - 1],
-        )
-
-    def ahead(y, offsets):
-        for zt in range(2):
-            rows = slice(8 * zt, 8 * zt + 8)
-            total = [tend_t[f, y, rows, :] for f in range(5)]
-            for k in offsets:
-                flux = plane_pair(y, k, zt)
-                for f in range(5):
-                    plane_flux[k - 1, f, y + 4, rows, :] = flux[f]
-                    total[f] = total[f] + flux[f]
-            for f in range(5):
-                tend_t[f, y, rows, :] = total[f]
-
-    def second_interior(y, carry):
-        ahead(y, range(1, 5))
-        return carry
-
-    lax.fori_loop(0, EDGE - 4, second_interior, 0)
-    for y in range(EDGE - 4, EDGE - 1):
-        ahead(y, range(1, EDGE - y))
+    z_copies = exchange_peaks(1, owners - 1, z_peers)
+    lax.fori_loop(EDGE // 2, EDGE, third_line, 0)
 
     copies[2].wait_recv()
     copies[3].wait_recv()
@@ -349,10 +361,10 @@
         line_tendency(nat, line, 0, store)
         return carry
 
-    lax.fori_loop(0, 2 * CAP, first_line, 0)
-
-    peak[2] = gather_peaks(1, owners - 1, y_copies)
-    z_copies = exchange_peaks(2, owners + 2, z_peers)
+    lax.fori_loop(0, CAP, first_line, 0)
+    peak[2] = gather_peaks(1, owners - 1, z_copies)
+    y_copies = exchange_peaks(2, owners + 2, y_peers)
+    lax.fori_loop(CAP, 2 * CAP, first_line, 0)
 
     copies[4].wait_recv()
     copies[5].wait_recv()
@@ -374,7 +386,7 @@
                 for f in range(5):
                     plane_flux[k - 1, f, y + 4, 8 * zt : 8 * zt + 8, :] = flux[f]
     for y in range(EDGE - 4, EDGE):
-        ahead(y, range(EDGE - y, 5))
+        ahead(y, range(EDGE - y, 5), False)
 
     def behind(y, carry):
         for zt in range(2):
@@ -388,30 +400,41 @@
 
     lax.fori_loop(0, EDGE, behind, 0)
 
-    top = jnp.max(gather_peaks(2, owners + 2, z_copies), keepdims=True)
-    time_step = COURANT / (EDGE * top)
     for f in range(5):
-        scale = 2.0 * time_step if f == 4 else time_step
         for half in range(2):
             part = tend_t[f, half * 8 : (half + 1) * 8, :, :].reshape(LANES, LANES).T
             for s in range(CAP):
-                out_ref[s, f, :, half * LANES : (half + 1) * LANES] = scale * (
-                    part[s * EDGE : (s + 1) * EDGE] + tend_x[f, 2 * s + half, :, :]
+                value = part[s * EDGE : (s + 1) * EDGE] + tend_x[f, 2 * s + half, :, :]
+                out_ref[s, f, :, half * LANES : (half + 1) * LANES] = (
+                    2.0 * value if f == 4 else value
                 )
+    info_ref[1] = jnp.full((8, LANES), owned, jnp.int32).astype(jnp.float32)
+    info_ref[0] = gather_peaks(2, owners + 2, y_copies)
     for copy in copies:
         copy.wait_send()
-
-
-def update_kernel(counts_ref, step_ref, sol_ref, reg_ref, new_sol_ref, new_reg_ref):
-    owned = counts_ref[lax.axis_index("block")]
-    size = step_ref.shape[0]
-    first = pl.program_id(0) * size
-    for s in range(size):
-        keep = first + s < owned
-        register = LOW_STORAGE_A[SECTION] * reg_ref[s] + step_ref[s]
-        state = sol_ref[s] + LOW_STORAGE_B[SECTION] * register
-        new_reg_ref[s] = jnp.where(keep, register, 0.0)
-        new_sol_ref[s] = jnp.where(keep, state, 0.0)
+    reg_load.wait()
+
+
+def update_kernel(tend_ref, info_ref, sol_ref, reg_ref, sol_hbm, reg_hbm, new_sol, new_reg, sems):
+    fastest = jnp.max(info_ref[0], axis=(0, 1), keepdims=True)
+    time_step = jnp.broadcast_to(COURANT / (EDGE * fastest), (EDGE, 2 * LANES))
+    owned = jnp.broadcast_to(info_ref[1, 0:1, 0:1], (EDGE, 2 * LANES))
+    copies = []
+    for s in range(CAP):
+        keep = owned > float(s)
+        for f in range(5):
+            register = LOW_STORAGE_A[SECTION] * reg_ref[s, f] + time_step * tend_ref[s, f]
+            state = sol_ref[s, f] + LOW_STORAGE_B[SECTION] * register
+            new_reg[s, f] = jnp.where(keep, register, 0.0)
+            new_sol[s, f] = jnp.where(keep, state, 0.0)
+        if s % 2 == 1:
+            part = pl.ds(s - 1, 2)
+            for i, (source, target) in enumerate(((new_reg, reg_hbm), (new_sol, sol_hbm))):
+                copy = pltpu.make_async_copy(source.at[part], target.at[part], sems.at[i, s // 2])
+                copy.start()
+                copies.append(copy)
+    for copy in copies:
+        copy.wait()
 
 
 def on_device(solution, register, counts):
@@ -419,7 +442,7 @@
     shape = blocks.shape
     f32 = jnp.float32
     scratch = [
-        pltpu.VMEM(shape, f32),
+        pltpu.SMEM((OWNERS,), jnp.int32),
         pltpu.VMEM((5, EDGE, EDGE, LANES), f32),
         pltpu.VMEM((2, 5, 4 * CAP, 2 * LANES), f32),
         pltpu.VMEM((2, 5, 4 * EDGE, LANES), f32),
@@ -435,35 +458,42 @@
         pltpu.VMEM((3, 8, LANES), f32),
         pltpu.VMEM((13, 8, LANES), f32),
         pltpu.SemaphoreType.DMA,
+        pltpu.SemaphoreType.DMA,
+        pltpu.SemaphoreType.DMA,
         pltpu.SemaphoreType.DMA((6,)),
         pltpu.SemaphoreType.DMA((6,)),
         pltpu.SemaphoreType.DMA((13,)),
         pltpu.SemaphoreType.DMA((13,)),
     ]
-    step = pl.pallas_call(
+    cells = jax.ShapeDtypeStruct(shape, f32)
+    tendency, info, state, past = pl.pallas_call(
         tendency_kernel,
-        out_shape=jax.ShapeDtypeStruct(shape, f32),
-        in_specs=[
-            pl.BlockSpec(memory_space=pltpu.SMEM),
-            pl.BlockSpec(memory_space=pl.ANY),
-        ],
-        out_specs=pl.BlockSpec(memory_space=pltpu.VMEM),
+        out_shape=[cells, jax.ShapeDtypeStruct((2, 8, LANES), f32), cells, cells],
+        in_specs=[pl.BlockSpec(memory_space=pltpu.HBM)] * 3,
+        out_specs=[pl.BlockSpec(memory_space=pltpu.VMEM)] * 4,
         scratch_shapes=scratch,
         compiler_params=pltpu.CompilerParams(
-            collective_id=0, has_side_effects=True, vmem_limit_bytes=40 * 2**20
+            collective_id=0, has_side_effects=True, vmem_limit_bytes=20 * 2**20
         ),
         name="tendency",
-    )(counts, blocks)
-    size = 2
-    spec = pl.BlockSpec((size,) + shape[1:], lambda i: (i, 0, 0, 0))
+    )(
+        pltpu.with_memory_space_constraint(counts, pltpu.HBM),
+        pltpu.with_memory_space_constraint(blocks, pltpu.HBM),
+        pltpu.with_memory_space_constraint(old_register, pltpu.HBM),
+    )
     new_solution, new_register = pl.pallas_call(
         update_kernel,
-        grid=(CAP // size,),
         out_shape=[jax.ShapeDtypeStruct(shape, f32)] * 2,
-        in_specs=[pl.BlockSpec(memory_space=pltpu.SMEM), spec, spec, spec],
-        out_specs=[spec, spec],
+        in_specs=[pl.BlockSpec(memory_space=pltpu.VMEM)] * 4,
+        out_specs=[pl.BlockSpec(memory_space=pltpu.HBM)] * 2,
+        scratch_shapes=[
+            pltpu.VMEM(shape, f32),
+            pltpu.VMEM(shape, f32),
+            pltpu.SemaphoreType.DMA((2, CAP // 2)),
+        ],
+        compiler_params=pltpu.CompilerParams(vmem_limit_bytes=8 * 2**20),
         name="update",
-    )(counts, step, blocks, old_register)
+    )(tendency, info, state, past)
     return (new_solution[None], new_register[None])
 
 

time: 30 us -> 23.3 us (0.78)
  Pallas kernels: 26.5 us -> 22.5 us
  local copies, waits for them, and re-layouts: 2.57 us -> 0 us
    pallas_call x2, Pallas kernels: 26.5 us -> 22.5 us  [the longest x1 21.2 us: on_device(): pl.pallas_call(tendency_kernel, out_shape=[cells, jax.ShapeDtypeStruct((2...]
    unnamed x6 -> x0, local copies, waits for them, and re-layouts: 2.57 us -> none
where the time goes in v2:
time: 23.3 us; the launch traced here: 23.2 us
  Pallas kernels  22.5 us (97%)
  between operations  0.64 us (3%)
    pallas_call x1, Pallas kernels, on_device(): pl.pallas_call(tendency_kernel, out_shape=[cells, jax.ShapeDtypeStruct((2...  21.2 us
    pallas_call x1, Pallas kernels, on_device(): pl.pallas_call(update_kernel, out_shape=[jax.ShapeDtypeStruct(shape, f32)...  1.29 us

profile of v2, /device:TPU:0, one launch (start us, length us, event | category | flops | bytes accessed | tf_op | source)
XLA Modules:
  0.0 23.2 jit_solution(303457839429861490)
XLA Ops:
  0.6 21.2 %tendency.1 = (f32[8,5,16,256]{3,2,1,0:T(8,128)S(1)}, f32[2,8,128]{2,1,0:T(8,128)S(1)}, f32[8,5,16,256]{3,2,1,0:T(8,128)S(1)}, f32[8,5,16,256]{3,2,1,0:T(8,128)S(1)}) custom-call(s32[8]{0:T(128)} %counts_hbm.1, f32[8,5,16,256]{3,2,1,0:T(8,128)} %bitcast.4, f32[8,5,16,256]{3,2,1,0:T(8,128)} %bitcast.5), custom_call_target="tpu_custom_call" | custom-call | tf_op jit(solution)/shard_map/tendency/pallas_call | solution.py:469
  21.9 1.3 %update.1 = (f32[8,5,16,256]{3,2,1,0:T(8,128)}, f32[8,5,16,256]{3,2,1,0:T(8,128)}) custom-call(f32[8,5,16,256]{3,2,1,0:T(8,128)S(1)} %get-tuple-element.8.tend_ref, f32[2,8,128]{2,1,0:T(8,128)S(1)} %get-tuple-element.9.info_ref, f32[8,5,16,256]{3,2,1,0:T(8,128)S(1)} %get-tuple-element.10.sol_ref, f32[8,5,16,256]{3,2,1,0:T(8,128)S(1)} %get-tuple-element.11.reg_ref), custom_call_target="tpu_custom_call" | custom-call | tf_op jit(solution)/shard_map/update/pallas_call | solution.py:484

commit v3 on v2

--- a/solution.py
+++ b/solution.py
@@ -32,6 +32,8 @@
 OWNERS = 8
 LANES = 128
 FIELDS = 8
+INNER = 2
+OUTER = 2
 
 
 def cell_fields(state):
@@ -128,8 +130,9 @@
 
     counts_load = pltpu.make_async_copy(counts_hbm, counts_ref, counts_sem)
     counts_load.start()
-    load = pltpu.make_async_copy(sol_hbm, sol, load_sem)
-    load.start()
+    loads = [pltpu.make_async_copy(sol_hbm.at[s], sol.at[s], load_sem.at[s]) for s in range(CAP)]
+    for load in loads:
+        load.start()
     barrier = pltpu.get_barrier_semaphore()
     everyone = [up_y, down_y] + y_peers + z_peers + block_peers
     for peer in everyone:
@@ -140,9 +143,9 @@
     owned = counts_ref[b]
     owned_below = counts_ref[lax.rem(b + owners - 1, owners)]
     lane_slot = lax.broadcasted_iota(jnp.int32, (8, LANES), 1) // EDGE
-    load.wait()
 
     def natural_fields(s, fastest):
+        pltpu.make_async_copy(sol_hbm.at[s], sol.at[s], load_sem.at[s]).wait()
         used = jnp.full((8, LANES), s, jnp.int32) < owned
         for half in range(2):
             for rt in range(2):
@@ -154,6 +157,8 @@
                 )
                 for f in range(FIELDS):
                     nat[f, 2 * s + half, 8 + 8 * rt : 16 + 8 * rt, :] = fields[f]
+                    if rt == 1:
+                        nat[f, 2 * s + half, 24:32, :] = fields[f]
                 speed = jnp.sqrt(v1 * v1 + v2 * v2 + v3 * v3) + jnp.sqrt(
                     HEAT_RATIO * pressure * inverse
                 )
@@ -166,15 +171,6 @@
         for s in range(CAP):
             pack_x[0, f, 4 * s : 4 * s + 4, :] = sol[s, f, 0:4, :]
             pack_x[1, f, 4 * s : 4 * s + 4, :] = sol[s, f, EDGE - 4 : EDGE, :]
-    for f in range(5):
-        for half in range(2):
-            part = sol[:, f, :, half * LANES : (half + 1) * LANES].reshape(LANES, LANES)
-            cons[f, half * 8 : (half + 1) * 8, :, :] = part.T.reshape(8, EDGE, LANES)
-    for f in range(5):
-        for y in range(EDGE):
-            pack_z[0, f, 4 * y : 4 * y + 4, :] = cons[f, y, 0:4, :]
-            pack_z[1, f, 4 * y : 4 * y + 4, :] = cons[f, y, EDGE - 4 : EDGE, :]
-
     def exchange_peaks(stage, first, peers):
         started = []
         for j, peer in enumerate(peers):
@@ -212,56 +208,98 @@
         copy.start()
         return copy
 
-    copies = [
-        send(0, pack_z.at[1], halo_z.at[0], up_z),
-        send(1, pack_z.at[0], halo_z.at[1], down_z),
-        send(2, pack_x.at[1], halo_x.at[0], up_x),
-        send(3, pack_x.at[0], halo_x.at[1], down_x),
-        send(4, cons.at[:, EDGE - 4 : EDGE], halo_y.at[0], up_y),
-        send(5, cons.at[:, 0:4], halo_y.at[1], down_y),
+    copies = {
+        2: send(2, pack_x.at[1], halo_x.at[0], up_x),
+        3: send(3, pack_x.at[0], halo_x.at[1], down_x),
+    }
+
+    for f in range(5):
+        for half in range(2):
+            part = sol[:, f, :, half * LANES : (half + 1) * LANES].reshape(LANES, LANES)
+            cons[f, half * 8 : (half + 1) * 8, :, :] = part.T.reshape(8, EDGE, LANES)
+    for f in range(5):
+        for y in range(EDGE):
+            pack_z[0, f, 4 * y : 4 * y + 4, :] = cons[f, y, 0:4, :]
+            pack_z[1, f, 4 * y : 4 * y + 4, :] = cons[f, y, EDGE - 4 : EDGE, :]
+
+    copies[4] = send(4, cons.at[:, EDGE - 4 : EDGE], halo_y.at[0], up_y)
+    copies[5] = send(5, cons.at[:, 0:4], halo_y.at[1], down_y)
+    copies[0] = send(0, pack_z.at[1], halo_z.at[0], up_z)
+    copies[1] = send(1, pack_z.at[0], halo_z.at[1], down_z)
+
+    def transposed_fields(group, carry):
+        for y in [2 * group + u for u in range(2)]:
+            for zt in range(2):
+                rows = slice(8 * zt, 8 * zt + 8)
+                fields = cell_fields([cons[f, y, rows, :] for f in range(5)])[0]
+                for f in range(FIELDS):
+                    tra[f, y + 4, 8 + 8 * zt : 16 + 8 * zt, :] = fields[f]
+                    if zt == 1:
+                        tra[f, y + 4, 24:32, :] = fields[f]
+        return carry
+
+    lax.fori_loop(0, (EDGE) // 2, transposed_fields, 0)
+
+
+    row = lax.broadcasted_iota(jnp.int32, (8, LANES), 0)
+    is_low = row < 4
+    inner = [jnp.where(row < 8 - k, FACTORS[k - 1], 0.0) for k in range(1, 5)]
+    outer = [
+        jnp.where(
+            is_low,
+            jnp.where(row < k, -FACTORS[k - 1], 0.0),
+            jnp.where(row >= 8 - k, FACTORS[k - 1], 0.0),
+        )
+        for k in range(1, 5)
     ]
-
-    def transposed_fields(y, carry):
-        for zt in range(2):
-            rows = slice(8 * zt, 8 * zt + 8)
-            fields = cell_fields([cons[f, y, rows, :] for f in range(5)])[0]
-            for f in range(FIELDS):
-                tra[f, y + 4, 8 + 8 * zt : 16 + 8 * zt, :] = fields[f]
-        return carry
-
-    lax.fori_loop(0, EDGE, transposed_fields, 0)
-
-
-    def line_tendency(ref, line, direction, store):
+    for u in range(2):
+        for k in range(4):
+            for f in range(5):
+                line_flux[u, k, f, 0:8, :] = jnp.zeros((8, LANES), jnp.float32)
+
+    def line_interior(ref, line, direction, u):
         left = [
             [ref[f, line, 8 + 8 * c : 16 + 8 * c, :] for f in range(FIELDS)] for c in range(2)
         ]
-        low = [ref[f, line, 4:8, :] for f in range(FIELDS)]
         total = [[None] * 5 for c in range(2)]
         for k in range(1, 5):
-            below = pair_flux(
-                low, [ref[f, line, 4 + k : 8 + k, :] for f in range(FIELDS)], direction, FACTORS[k - 1]
-            )
-            for f in range(5):
-                line_flux[k - 1, f, 4:8, :] = below[f]
             for c in range(2):
                 at = 8 + 8 * c
                 flux = pair_flux(
                     left[c],
                     [ref[f, line, at + k : at + 8 + k, :] for f in range(FIELDS)],
                     direction,
-                    FACTORS[k - 1],
+                    inner[k - 1] if c == 1 else FACTORS[k - 1],
                 )
                 for f in range(5):
-                    line_flux[k - 1, f, at : at + 8, :] = flux[f]
+                    line_flux[u, k - 1, f, at : at + 8, :] = flux[f]
                     total[c][f] = flux[f] if k == 1 else total[c][f] + flux[f]
             for c in range(2):
                 at = 8 + 8 * c
                 for f in range(5):
-                    total[c][f] = total[c][f] - line_flux[k - 1, f, at - k : at + 8 - k, :]
-        for c in range(2):
-            for f in range(5):
-                store(f, c, total[c][f])
+                    total[c][f] = total[c][f] - line_flux[u, k - 1, f, at - k : at + 8 - k, :]
+        return total
+
+    def line_boundary(ref, line, direction):
+        first_rows = [ref[f, line, 8:16, :] for f in range(FIELDS)]
+        last_rows = [ref[f, line, 16:24, :] for f in range(FIELDS)]
+        total = [None] * 5
+        for k in range(1, 5):
+            flux = pair_flux(
+                [
+                    jnp.where(is_low, ref[f, line, 8 - k : 16 - k, :], last_rows[f])
+                    for f in range(FIELDS)
+                ],
+                [
+                    jnp.where(is_low, first_rows[f], ref[f, line, 16 + k : 24 + k, :])
+                    for f in range(FIELDS)
+                ],
+                direction,
+                outer[k - 1],
+            )
+            for f in range(5):
+                total[f] = flux[f] if k == 1 else total[f] + flux[f]
+        return [jnp.where(is_low, t, 0.0) for t in total], [jnp.where(is_low, 0.0, t) for t in total]
 
     def plane_pair(y, k, zt):
         rows = slice(8 + 8 * zt, 16 + 8 * zt)
@@ -272,10 +310,10 @@
             FACTORS[k - 1],
         )
 
-    def ahead(y, offsets, fresh):
+    def ahead(y, offsets):
         for zt in range(2):
             rows = slice(8 * zt, 8 * zt + 8)
-            total = [None if fresh else tend_t[f, y, rows, :] for f in range(5)]
+            total = [None] * 5
             for k in offsets:
                 flux = plane_pair(y, k, zt)
                 for f in range(5):
@@ -285,120 +323,159 @@
                 tend_t[f, y, rows, :] = total[f]
 
     def second_interior(y, carry):
-        ahead(y, range(1, 5), True)
+        ahead(y, range(1, 5))
         return carry
 
     lax.fori_loop(0, EDGE - 4, second_interior, 0)
     for y in range(EDGE - 4, EDGE - 1):
-        ahead(y, range(1, EDGE - y), True)
+        ahead(y, range(1, EDGE - y))
     for f in range(5):
         tend_t[f, EDGE - 1, :, :] = jnp.zeros((EDGE, LANES), jnp.float32)
 
+    peak[1] = gather_peaks(0, 0, block_copies)
+    z_copies = exchange_peaks(1, owners - 1, z_peers)
+
+    def behind(y, offsets):
+        for zt in range(2):
+            rows = slice(8 * zt, 8 * zt + 8)
+            for f in range(5):
+                total = tend_t[f, y, rows, :]
+                for k in offsets:
+                    total = total - plane_flux[k - 1, f, y + 4 - k, rows, :]
+                tend_t[f, y, rows, :] = total
+
+    def second_behind(y, carry):
+        behind(y, range(1, 5))
+        return carry
+
+    for y in range(1, 4):
+        behind(y, range(1, y + 1))
+    lax.fori_loop(4, EDGE, second_behind, 0)
+
+    def third_line(i, carry):
+        for u in range(INNER):
+            y = INNER * i + u
+            total = line_interior(tra, y + 4, 2, u)
+            for f in range(5):
+                for c in range(2):
+                    rows = slice(8 * c, 8 * c + 8)
+                    tend_t[f, y, rows, :] = tend_t[f, y, rows, :] + total[c][f]
+        return carry
+
+    def first_line(i, carry):
+        for u in range(INNER):
+            line = INNER * i + u
+            total = line_interior(nat, line, 0, u)
+            for f in range(5):
+                for c in range(2):
+                    tend_x[f, line, 8 * c : 8 * c + 8, :] = total[c][f]
+        return carry
+
+    lax.fori_loop(0, EDGE // INNER, third_line, 0)
+    lax.fori_loop(0, CAP // INNER, first_line, 0)
+    peak[2] = gather_peaks(1, owners - 1, z_copies)
+    y_copies = exchange_peaks(2, owners + 2, y_peers)
+    lax.fori_loop(CAP // INNER, 2 * CAP // INNER, first_line, 0)
+
     copies[0].wait_recv()
     copies[1].wait_recv()
 
-    def third_halo(i, carry):
-        rows = pl.ds(pl.multiple_of(8 * i, 8), 8)
-        lower, upper = [], []
-        for f in range(5):
-            below = jnp.where(lane_slot == owned_below - 1, halo_z[0, f, rows, :], 0.0)
-            above = jnp.where(lane_slot == 0, halo_z[1, f, rows, :], 0.0)
-            for shift in (16, 32, 64):
-                below = below + pltpu.roll(below, shift, 1)
-                above = above + pltpu.roll(above, shift, 1)
-            lower.append(
-                jnp.where(lane_slot == 0, below, pltpu.roll(pack_z[1, f, rows, :], EDGE, 1))
-            )
-            upper.append(
-                jnp.where(
-                    lane_slot == owned - 1, above, pltpu.roll(pack_z[0, f, rows, :], LANES - EDGE, 1)
+    def third_halo(group, carry):
+        for i in [4 * group + u for u in range(4)]:
+            rows = pl.ds(pl.multiple_of(8 * i, 8), 8)
+            lower, upper = [], []
+            for f in range(5):
+                below = jnp.where(lane_slot == owned_below - 1, halo_z[0, f, rows, :], 0.0)
+                above = jnp.where(lane_slot == 0, halo_z[1, f, rows, :], 0.0)
+                for shift in (16, 32, 64):
+                    below = below + pltpu.roll(below, shift, 1)
+                    above = above + pltpu.roll(above, shift, 1)
+                lower.append(
+                    jnp.where(lane_slot == 0, below, pltpu.roll(pack_z[1, f, rows, :], EDGE, 1))
                 )
-            )
-        lower, _ = cell_fields(lower)
-        upper, _ = cell_fields(upper)
-        for f in range(FIELDS):
-            for j in range(2):
-                tra[f, 2 * i + j + 4, 4:8, :] = lower[f][4 * j : 4 * j + 4]
-                tra[f, 2 * i + j + 4, 24:28, :] = upper[f][4 * j : 4 * j + 4]
-        return carry
-
-    lax.fori_loop(0, EDGE // 2, third_halo, 0)
-
-    def third_line(y, carry):
-        def store(f, c, value):
-            rows = slice(8 * c, 8 * c + 8)
-            tend_t[f, y, rows, :] = tend_t[f, y, rows, :] + value
-
-        line_tendency(tra, y + 4, 2, store)
-        return carry
-
-    lax.fori_loop(0, EDGE // 2, third_line, 0)
-    peak[1] = gather_peaks(0, 0, block_copies)
-    z_copies = exchange_peaks(1, owners - 1, z_peers)
-    lax.fori_loop(EDGE // 2, EDGE, third_line, 0)
-
+                upper.append(
+                    jnp.where(
+                        lane_slot == owned - 1, above, pltpu.roll(pack_z[0, f, rows, :], LANES - EDGE, 1)
+                    )
+                )
+            lower, _ = cell_fields(lower)
+            upper, _ = cell_fields(upper)
+            for f in range(FIELDS):
+                for j in range(2):
+                    tra[f, 2 * i + j + 4, 4:8, :] = lower[f][4 * j : 4 * j + 4]
+                    tra[f, 2 * i + j + 4, 24:28, :] = upper[f][4 * j : 4 * j + 4]
+        return carry
+
+    lax.fori_loop(0, (EDGE // 2) // 4, third_halo, 0)
+
+    def third_boundary(i, carry):
+        for u in range(OUTER):
+            y = OUTER * i + u
+            total = line_boundary(tra, y + 4, 2)
+            for f in range(5):
+                for c in range(2):
+                    rows = slice(8 * c, 8 * c + 8)
+                    tend_t[f, y, rows, :] = tend_t[f, y, rows, :] + total[c][f]
+        return carry
+
+    lax.fori_loop(0, EDGE // OUTER, third_boundary, 0)
     copies[2].wait_recv()
     copies[3].wait_recv()
 
-    def first_halo(i, carry):
-        rows = pl.ds(pl.multiple_of(8 * i, 8), 8)
-        for side in range(2):
-            at = 4 if side == 0 else 24
-            for half in range(2):
-                lanes = slice(half * LANES, (half + 1) * LANES)
-                fields, _ = cell_fields([halo_x[side, f, rows, lanes] for f in range(5)])
-                for f in range(FIELDS):
-                    for j in range(2):
-                        nat[f, 2 * (2 * i + j) + half, at : at + 4, :] = fields[f][4 * j : 4 * j + 4]
-        return carry
-
-    lax.fori_loop(0, CAP // 2, first_halo, 0)
-
-    def first_line(line, carry):
-        def store(f, c, value):
-            tend_x[f, line, 8 * c : 8 * c + 8, :] = value
-
-        line_tendency(nat, line, 0, store)
-        return carry
-
-    lax.fori_loop(0, CAP, first_line, 0)
-    peak[2] = gather_peaks(1, owners - 1, z_copies)
-    y_copies = exchange_peaks(2, owners + 2, y_peers)
-    lax.fori_loop(CAP, 2 * CAP, first_line, 0)
-
+    def first_halo(group, carry):
+        for i in [2 * group + u for u in range(2)]:
+            rows = pl.ds(pl.multiple_of(8 * i, 8), 8)
+            for side in range(2):
+                at = 4 if side == 0 else 24
+                for half in range(2):
+                    lanes = slice(half * LANES, (half + 1) * LANES)
+                    fields, _ = cell_fields([halo_x[side, f, rows, lanes] for f in range(5)])
+                    for f in range(FIELDS):
+                        for j in range(2):
+                            nat[f, 2 * (2 * i + j) + half, at : at + 4, :] = fields[f][4 * j : 4 * j + 4]
+        return carry
+
+    lax.fori_loop(0, (CAP // 2) // 2, first_halo, 0)
+
+    def first_boundary(i, carry):
+        for u in range(OUTER):
+            line = OUTER * i + u
+            total = line_boundary(nat, line, 0)
+            for f in range(5):
+                for c in range(2):
+                    rows = slice(8 * c, 8 * c + 8)
+                    tend_x[f, line, rows, :] = tend_x[f, line, rows, :] + total[c][f]
+        return carry
+
+    lax.fori_loop(0, 2 * CAP // OUTER, first_boundary, 0)
     copies[4].wait_recv()
     copies[5].wait_recv()
 
-    def second_halo(y, carry):
-        for side in range(2):
-            for zt in range(2):
-                rows = slice(8 * zt, 8 * zt + 8)
-                fields, _ = cell_fields([halo_y[side, f, y, rows, :] for f in range(5)])
-                for f in range(FIELDS):
-                    tra[f, y + 20 * side, 8 + 8 * zt : 16 + 8 * zt, :] = fields[f]
-        return carry
-
-    lax.fori_loop(0, 4, second_halo, 0)
-    for y in range(-4, 0):
-        for k in range(-y, 5):
-            for zt in range(2):
-                flux = plane_pair(y, k, zt)
-                for f in range(5):
-                    plane_flux[k - 1, f, y + 4, 8 * zt : 8 * zt + 8, :] = flux[f]
-    for y in range(EDGE - 4, EDGE):
-        ahead(y, range(EDGE - y, 5), False)
-
-    def behind(y, carry):
+    def second_halo(group, carry):
+        for y in [2 * group + u for u in range(2)]:
+            for side in range(2):
+                for zt in range(2):
+                    rows = slice(8 * zt, 8 * zt + 8)
+                    fields, _ = cell_fields([halo_y[side, f, y, rows, :] for f in range(5)])
+                    for f in range(FIELDS):
+                        tra[f, y + 20 * side, 8 + 8 * zt : 16 + 8 * zt, :] = fields[f]
+        return carry
+
+    lax.fori_loop(0, (4) // 2, second_halo, 0)
+    for y in range(4):
         for zt in range(2):
             rows = slice(8 * zt, 8 * zt + 8)
-            for f in range(5):
-                total = tend_t[f, y, rows, :]
-                for k in range(1, 5):
-                    total = total - plane_flux[k - 1, f, y + 4 - k, rows, :]
-                tend_t[f, y, rows, :] = total
-        return carry
-
-    lax.fori_loop(0, EDGE, behind, 0)
+            low = [tend_t[f, y, rows, :] for f in range(5)]
+            high = [tend_t[f, y + EDGE - 4, rows, :] for f in range(5)]
+            for k in range(y + 1, 5):
+                flux = plane_pair(y - k, k, zt)
+                low = [low[f] - flux[f] for f in range(5)]
+            for k in range(4 - y, 5):
+                flux = plane_pair(y + EDGE - 4, k, zt)
+                high = [high[f] + flux[f] for f in range(5)]
+            for f in range(5):
+                tend_t[f, y, rows, :] = low[f]
+                tend_t[f, y + EDGE - 4, rows, :] = high[f]
 
     for f in range(5):
         for half in range(2):
@@ -410,7 +487,7 @@
                 )
     info_ref[1] = jnp.full((8, LANES), owned, jnp.int32).astype(jnp.float32)
     info_ref[0] = gather_peaks(2, owners + 2, y_copies)
-    for copy in copies:
+    for copy in copies.values():
         copy.wait_send()
     reg_load.wait()
 
@@ -451,13 +528,13 @@
         pltpu.VMEM((2, 5, 4 * EDGE, LANES), f32),
         pltpu.VMEM((FIELDS, 2 * CAP, 32, LANES), f32),
         pltpu.VMEM((FIELDS, EDGE + 8, 32, LANES), f32),
-        pltpu.VMEM((4, 5, 24, LANES), f32),
+        pltpu.VMEM((2, 4, 5, 24, LANES), f32),
         pltpu.VMEM((4, 5, EDGE + 4, EDGE, LANES), f32),
         pltpu.VMEM((5, 2 * CAP, EDGE, LANES), f32),
         pltpu.VMEM((5, EDGE, EDGE, LANES), f32),
         pltpu.VMEM((3, 8, LANES), f32),
         pltpu.VMEM((13, 8, LANES), f32),
-        pltpu.SemaphoreType.DMA,
+        pltpu.SemaphoreType.DMA((CAP,)),
         pltpu.SemaphoreType.DMA,
         pltpu.SemaphoreType.DMA,
         pltpu.SemaphoreType.DMA((6,)),

time: 23.3 us -> 21.3 us (0.914)
  the two profiles are of different devices: /device:TPU:0 before, /device:TPU:1 now
where the time goes in v3:
time: 21.3 us; the launch traced here: 21.2 us
  Pallas kernels  20.5 us (96%)
  between operations  0.64 us (3%)
    pallas_call x1, Pallas kernels, on_device(): pl.pallas_call(tendency_kernel, out_shape=[cells, jax.ShapeDtypeStruct((2...  19.3 us
    pallas_call x1, Pallas kernels, on_device(): pl.pallas_call(update_kernel, out_shape=[jax.ShapeDtypeStruct(shape, f32)...  1.29 us

profile of v3, /device:TPU:1, one launch (start us, length us, event | category | flops | bytes accessed | tf_op | source)
XLA Modules:
  0.0 21.2 jit_solution(8732329884694706071)
XLA Ops:
  0.6 19.3 %tendency.1 = (f32[8,5,16,256]{3,2,1,0:T(8,128)S(1)}, f32[2,8,128]{2,1,0:T(8,128)S(1)}, f32[8,5,16,256]{3,2,1,0:T(8,128)S(1)}, f32[8,5,16,256]{3,2,1,0:T(8,128)S(1)}) custom-call(s32[8]{0:T(128)} %counts_hbm.1, f32[8,5,16,256]{3,2,1,0:T(8,128)} %bitcast.4, f32[8,5,16,256]{3,2,1,0:T(8,128)} %bitcast.5), custom_call_target="tpu_custom_call" | custom-call | tf_op jit(solution)/shard_map/tendency/pallas_call | solution.py:546
  19.9 1.3 %update.1 = (f32[8,5,16,256]{3,2,1,0:T(8,128)}, f32[8,5,16,256]{3,2,1,0:T(8,128)}) custom-call(f32[8,5,16,256]{3,2,1,0:T(8,128)S(1)} %get-tuple-element.8.tend_ref, f32[2,8,128]{2,1,0:T(8,128)S(1)} %get-tuple-element.9.info_ref, f32[8,5,16,256]{3,2,1,0:T(8,128)S(1)} %get-tuple-element.10.sol_ref, f32[8,5,16,256]{3,2,1,0:T(8,128)S(1)} %get-tuple-element.11.reg_ref), custom_call_target="tpu_custom_call" | custom-call | tf_op jit(solution)/shard_map/update/pallas_call | solution.py:561

commit v4 on v3

--- a/solution.py
+++ b/solution.py
@@ -104,6 +104,7 @@
     plane_flux,
     tend_x,
     tend_t,
+    edge_t,
     peak,
     peak_in,
     load_sem,
@@ -171,6 +172,15 @@
         for s in range(CAP):
             pack_x[0, f, 4 * s : 4 * s + 4, :] = sol[s, f, 0:4, :]
             pack_x[1, f, 4 * s : 4 * s + 4, :] = sol[s, f, EDGE - 4 : EDGE, :]
+    for f in range(5):
+        for half in range(2):
+            part = sol[:, f, :, half * LANES : (half + 1) * LANES].reshape(LANES, LANES)
+            cons[f, half * 8 : (half + 1) * 8, :, :] = part.T.reshape(8, EDGE, LANES)
+    for f in range(5):
+        for y in range(EDGE):
+            pack_z[0, f, 4 * y : 4 * y + 4, :] = cons[f, y, 0:4, :]
+            pack_z[1, f, 4 * y : 4 * y + 4, :] = cons[f, y, EDGE - 4 : EDGE, :]
+
     def exchange_peaks(stage, first, peers):
         started = []
         for j, peer in enumerate(peers):
@@ -193,9 +203,6 @@
             value = jnp.maximum(value, peak_in[first + j])
         return value
 
-    pl.semaphore_wait(barrier, len(everyone))
-    block_copies = exchange_peaks(0, 0, block_peers)
-
     def send(index, source, target, peer):
         copy = pltpu.make_async_remote_copy(
             src_ref=source,
@@ -208,22 +215,14 @@
         copy.start()
         return copy
 
+    pl.semaphore_wait(barrier, len(everyone))
     copies = {
-        2: send(2, pack_x.at[1], halo_x.at[0], up_x),
-        3: send(3, pack_x.at[0], halo_x.at[1], down_x),
+        4: send(4, cons.at[:, EDGE - 4 : EDGE], halo_y.at[0], up_y),
+        5: send(5, cons.at[:, 0:4], halo_y.at[1], down_y),
     }
-
-    for f in range(5):
-        for half in range(2):
-            part = sol[:, f, :, half * LANES : (half + 1) * LANES].reshape(LANES, LANES)
-            cons[f, half * 8 : (half + 1) * 8, :, :] = part.T.reshape(8, EDGE, LANES)
-    for f in range(5):
-        for y in range(EDGE):
-            pack_z[0, f, 4 * y : 4 * y + 4, :] = cons[f, y, 0:4, :]
-            pack_z[1, f, 4 * y : 4 * y + 4, :] = cons[f, y, EDGE - 4 : EDGE, :]
-
-    copies[4] = send(4, cons.at[:, EDGE - 4 : EDGE], halo_y.at[0], up_y)
-    copies[5] = send(5, cons.at[:, 0:4], halo_y.at[1], down_y)
+    block_copies = exchange_peaks(0, 0, block_peers)
+    copies[2] = send(2, pack_x.at[1], halo_x.at[0], up_x)
+    copies[3] = send(3, pack_x.at[0], halo_x.at[1], down_x)
     copies[0] = send(0, pack_z.at[1], halo_z.at[0], up_z)
     copies[1] = send(1, pack_z.at[0], halo_z.at[1], down_z)
 
@@ -448,6 +447,14 @@
         return carry
 
     lax.fori_loop(0, 2 * CAP // OUTER, first_boundary, 0)
+    for f in range(5):
+        for half in range(2):
+            part = tend_t[f, half * 8 : (half + 1) * 8, :, :].reshape(LANES, LANES).T
+            for s in range(CAP):
+                value = part[s * EDGE : (s + 1) * EDGE] + tend_x[f, 2 * s + half, :, :]
+                out_ref[s, f, :, half * LANES : (half + 1) * LANES] = (
+                    2.0 * value if f == 4 else value
+                )
     copies[4].wait_recv()
     copies[5].wait_recv()
 
@@ -465,26 +472,28 @@
     for y in range(4):
         for zt in range(2):
             rows = slice(8 * zt, 8 * zt + 8)
-            low = [tend_t[f, y, rows, :] for f in range(5)]
-            high = [tend_t[f, y + EDGE - 4, rows, :] for f in range(5)]
+            low, high = [None] * 5, [None] * 5
             for k in range(y + 1, 5):
                 flux = plane_pair(y - k, k, zt)
-                low = [low[f] - flux[f] for f in range(5)]
+                low = [-flux[f] if low[f] is None else low[f] - flux[f] for f in range(5)]
             for k in range(4 - y, 5):
                 flux = plane_pair(y + EDGE - 4, k, zt)
-                high = [high[f] + flux[f] for f in range(5)]
-            for f in range(5):
-                tend_t[f, y, rows, :] = low[f]
-                tend_t[f, y + EDGE - 4, rows, :] = high[f]
-
+                high = [flux[f] if high[f] is None else high[f] + flux[f] for f in range(5)]
+            for f in range(5):
+                edge_t[f, y, rows, :] = low[f]
+                edge_t[f, y + 4, rows, :] = high[f]
+
+    left_lanes = lax.broadcasted_iota(jnp.int32, (EDGE, LANES), 1) < LANES // 2
     for f in range(5):
-        for half in range(2):
-            part = tend_t[f, half * 8 : (half + 1) * 8, :, :].reshape(LANES, LANES).T
-            for s in range(CAP):
-                value = part[s * EDGE : (s + 1) * EDGE] + tend_x[f, 2 * s + half, :, :]
-                out_ref[s, f, :, half * LANES : (half + 1) * LANES] = (
-                    2.0 * value if f == 4 else value
-                )
+        part = edge_t[f].reshape(LANES, LANES).T
+        for s in range(CAP):
+            value = part[s * EDGE : (s + 1) * EDGE]
+            if f == 4:
+                value = 2.0 * value
+            for half in range(2):
+                lanes = slice(half * LANES, (half + 1) * LANES)
+                mine = left_lanes if half == 0 else jnp.logical_not(left_lanes)
+                out_ref[s, f, :, lanes] = out_ref[s, f, :, lanes] + jnp.where(mine, value, 0.0)
     info_ref[1] = jnp.full((8, LANES), owned, jnp.int32).astype(jnp.float32)
     info_ref[0] = gather_peaks(2, owners + 2, y_copies)
     for copy in copies.values():
@@ -532,6 +541,7 @@
         pltpu.VMEM((4, 5, EDGE + 4, EDGE, LANES), f32),
         pltpu.VMEM((5, 2 * CAP, EDGE, LANES), f32),
         pltpu.VMEM((5, EDGE, EDGE, LANES), f32),
+        pltpu.VMEM((5, 8, EDGE, LANES), f32),
         pltpu.VMEM((3, 8, LANES), f32),
         pltpu.VMEM((13, 8, LANES), f32),
         pltpu.SemaphoreType.DMA((CAP,)),

time: 21.3 us -> 21.1 us (level)
  no operation moved by 1% of the time
where the time goes in v4:
time: 21.1 us; the launch traced here: 21 us
  Pallas kernels  20.3 us (96%)
  between operations  0.64 us (3%)
    pallas_call x1, Pallas kernels, on_device(): pl.pallas_call(tendency_kernel, out_shape=[cells, jax.ShapeDtypeStruct((2...  19.1 us
    pallas_call x1, Pallas kernels, on_device(): pl.pallas_call(update_kernel, out_shape=[jax.ShapeDtypeStruct(shape, f32)...  1.29 us

profile of v4, /device:TPU:1, one launch (start us, length us, event | category | flops | bytes accessed | tf_op | source)
XLA Modules:
  0.0 21.0 jit_solution(12403101972999477873)
XLA Ops:
  0.6 19.1 %tendency.1 = (f32[8,5,16,256]{3,2,1,0:T(8,128)S(1)}, f32[2,8,128]{2,1,0:T(8,128)S(1)}, f32[8,5,16,256]{3,2,1,0:T(8,128)S(1)}, f32[8,5,16,256]{3,2,1,0:T(8,128)S(1)}) custom-call(s32[8]{0:T(128)} %counts_hbm.1, f32[8,5,16,256]{3,2,1,0:T(8,128)} %bitcast.4, f32[8,5,16,256]{3,2,1,0:T(8,128)} %bitcast.5), custom_call_target="tpu_custom_call" | custom-call | tf_op jit(solution)/shard_map/tendency/pallas_call | solution.py:556
  19.7 1.3 %update.1 = (f32[8,5,16,256]{3,2,1,0:T(8,128)}, f32[8,5,16,256]{3,2,1,0:T(8,128)}) custom-call(f32[8,5,16,256]{3,2,1,0:T(8,128)S(1)} %get-tuple-element.8.tend_ref, f32[2,8,128]{2,1,0:T(8,128)S(1)} %get-tuple-element.9.info_ref, f32[8,5,16,256]{3,2,1,0:T(8,128)S(1)} %get-tuple-element.10.sol_ref, f32[8,5,16,256]{3,2,1,0:T(8,128)S(1)} %get-tuple-element.11.reg_ref), custom_call_target="tpu_custom_call" | custom-call | tf_op jit(solution)/shard_map/update/pallas_call | solution.py:571

commit v5 on v4

--- a/solution.py
+++ b/solution.py
@@ -172,15 +172,6 @@
         for s in range(CAP):
             pack_x[0, f, 4 * s : 4 * s + 4, :] = sol[s, f, 0:4, :]
             pack_x[1, f, 4 * s : 4 * s + 4, :] = sol[s, f, EDGE - 4 : EDGE, :]
-    for f in range(5):
-        for half in range(2):
-            part = sol[:, f, :, half * LANES : (half + 1) * LANES].reshape(LANES, LANES)
-            cons[f, half * 8 : (half + 1) * 8, :, :] = part.T.reshape(8, EDGE, LANES)
-    for f in range(5):
-        for y in range(EDGE):
-            pack_z[0, f, 4 * y : 4 * y + 4, :] = cons[f, y, 0:4, :]
-            pack_z[1, f, 4 * y : 4 * y + 4, :] = cons[f, y, EDGE - 4 : EDGE, :]
-
     def exchange_peaks(stage, first, peers):
         started = []
         for j, peer in enumerate(peers):
@@ -216,11 +207,20 @@
         return copy
 
     pl.semaphore_wait(barrier, len(everyone))
+    block_copies = exchange_peaks(0, 0, block_peers)
+    for f in range(5):
+        for half in range(2):
+            part = sol[:, f, :, half * LANES : (half + 1) * LANES].reshape(LANES, LANES)
+            cons[f, half * 8 : (half + 1) * 8, :, :] = part.T.reshape(8, EDGE, LANES)
+    for f in range(5):
+        for y in range(EDGE):
+            pack_z[0, f, 4 * y : 4 * y + 4, :] = cons[f, y, 0:4, :]
+            pack_z[1, f, 4 * y : 4 * y + 4, :] = cons[f, y, EDGE - 4 : EDGE, :]
+
     copies = {
         4: send(4, cons.at[:, EDGE - 4 : EDGE], halo_y.at[0], up_y),
         5: send(5, cons.at[:, 0:4], halo_y.at[1], down_y),
     }
-    block_copies = exchange_peaks(0, 0, block_peers)
     copies[2] = send(2, pack_x.at[1], halo_x.at[0], up_x)
     copies[3] = send(3, pack_x.at[0], halo_x.at[1], down_x)
     copies[0] = send(0, pack_z.at[1], halo_z.at[0], up_z)

time: 21.1 us -> 21.1 us (level)
  no operation moved by 1% of the time
where the time goes in v5:
time: 21.1 us; the launch traced here: 21 us
  Pallas kernels  20.3 us (96%)
  between operations  0.64 us (3%)
    pallas_call x1, Pallas kernels, on_device(): pl.pallas_call(tendency_kernel, out_shape=[cells, jax.ShapeDtypeStruct((2...  19 us
    pallas_call x1, Pallas kernels, on_device(): pl.pallas_call(update_kernel, out_shape=[jax.ShapeDtypeStruct(shape, f32)...  1.29 us

profile of v5, /device:TPU:1, one launch (start us, length us, event | category | flops | bytes accessed | tf_op | source)
XLA Modules:
  0.0 21.0 jit_solution(12333029989543686213)
XLA Ops:
  0.6 19.0 %tendency.1 = (f32[8,5,16,256]{3,2,1,0:T(8,128)S(1)}, f32[2,8,128]{2,1,0:T(8,128)S(1)}, f32[8,5,16,256]{3,2,1,0:T(8,128)S(1)}, f32[8,5,16,256]{3,2,1,0:T(8,128)S(1)}) custom-call(s32[8]{0:T(128)} %counts_hbm.1, f32[8,5,16,256]{3,2,1,0:T(8,128)} %bitcast.4, f32[8,5,16,256]{3,2,1,0:T(8,128)} %bitcast.5), custom_call_target="tpu_custom_call" | custom-call | tf_op jit(solution)/shard_map/tendency/pallas_call | solution.py:556
  19.7 1.3 %update.1 = (f32[8,5,16,256]{3,2,1,0:T(8,128)}, f32[8,5,16,256]{3,2,1,0:T(8,128)}) custom-call(f32[8,5,16,256]{3,2,1,0:T(8,128)S(1)} %get-tuple-element.8.tend_ref, f32[2,8,128]{2,1,0:T(8,128)S(1)} %get-tuple-element.9.info_ref, f32[8,5,16,256]{3,2,1,0:T(8,128)S(1)} %get-tuple-element.10.sol_ref, f32[8,5,16,256]{3,2,1,0:T(8,128)S(1)} %get-tuple-element.11.reg_ref), custom_call_target="tpu_custom_call" | custom-call | tf_op jit(solution)/shard_map/update/pallas_call | solution.py:571

commit v6 on v4

--- a/solution.py
+++ b/solution.py
@@ -331,9 +331,6 @@
     for f in range(5):
         tend_t[f, EDGE - 1, :, :] = jnp.zeros((EDGE, LANES), jnp.float32)
 
-    peak[1] = gather_peaks(0, 0, block_copies)
-    z_copies = exchange_peaks(1, owners - 1, z_peers)
-
     def behind(y, offsets):
         for zt in range(2):
             rows = slice(8 * zt, 8 * zt + 8)
@@ -350,6 +347,9 @@
     for y in range(1, 4):
         behind(y, range(1, y + 1))
     lax.fori_loop(4, EDGE, second_behind, 0)
+
+    peak[1] = gather_peaks(0, 0, block_copies)
+    z_copies = exchange_peaks(1, owners - 1, z_peers)
 
     def third_line(i, carry):
         for u in range(INNER):

time: 21.1 us -> 21.1 us (level)
  no operation moved by 1% of the time
where the time goes in v6:
time: 21.1 us; the launch traced here: 21 us
  Pallas kernels  20.3 us (96%)
  between operations  0.64 us (3%)
    pallas_call x1, Pallas kernels, on_device(): pl.pallas_call(tendency_kernel, out_shape=[cells, jax.ShapeDtypeStruct((2...  19 us
    pallas_call x1, Pallas kernels, on_device(): pl.pallas_call(update_kernel, out_shape=[jax.ShapeDtypeStruct(shape, f32)...  1.29 us

profile of v6, /device:TPU:1, one launch (start us, length us, event | category | flops | bytes accessed | tf_op | source)
XLA Modules:
  0.0 21.0 jit_solution(5431445984155705612)
XLA Ops:
  0.6 19.0 %tendency.1 = (f32[8,5,16,256]{3,2,1,0:T(8,128)S(1)}, f32[2,8,128]{2,1,0:T(8,128)S(1)}, f32[8,5,16,256]{3,2,1,0:T(8,128)S(1)}, f32[8,5,16,256]{3,2,1,0:T(8,128)S(1)}) custom-call(s32[8]{0:T(128)} %counts_hbm.1, f32[8,5,16,256]{3,2,1,0:T(8,128)} %bitcast.4, f32[8,5,16,256]{3,2,1,0:T(8,128)} %bitcast.5), custom_call_target="tpu_custom_call" | custom-call | tf_op jit(solution)/shard_map/tendency/pallas_call | solution.py:556
  19.7 1.3 %update.1 = (f32[8,5,16,256]{3,2,1,0:T(8,128)}, f32[8,5,16,256]{3,2,1,0:T(8,128)}) custom-call(f32[8,5,16,256]{3,2,1,0:T(8,128)S(1)} %get-tuple-element.8.tend_ref, f32[2,8,128]{2,1,0:T(8,128)S(1)} %get-tuple-element.9.info_ref, f32[8,5,16,256]{3,2,1,0:T(8,128)S(1)} %get-tuple-element.10.sol_ref, f32[8,5,16,256]{3,2,1,0:T(8,128)S(1)} %get-tuple-element.11.reg_ref), custom_call_target="tpu_custom_call" | custom-call | tf_op jit(solution)/shard_map/update/pallas_call | solution.py:571
